TPU v7x, 512 devices: a whole 4x8x8 slice. The times are simulated.
512 devices in a mesh: vox: 64 (over z, x, core), ch: 8 (over y).
Axes of the slice: x: 4, y: 8, z: 8, core: 2. Of those that a mesh axis runs over, the one named last changes fastest.
Arguments:
- features: bfloat16 [128, 262144], P('ch', 'vox'), may hold values from -6 to 6
- conv_weight: bfloat16 [27, 128, 128], P(None, None, 'ch'), may hold values from -0.109375 to 0.109375
- qkv_weight: bfloat16 [3, 128, 128], P(None, None, 'ch')
- out_weight: bfloat16 [128, 128], P('ch'), may hold values from -0.5 to 0.5
- cotangent: bfloat16 [128, 65536], P('ch', 'vox'), may hold values from -6 to 6
- neighbours: int32 [27, 262144], P(None, 'vox'), may hold values from -1 to 4607, as said below
- send_slot: int32 [262144], P('vox'), may hold values from -1 to 1023, as said below
- recv_slot: int32 [65536], P('vox'), may hold values from -1 to 1023, as said below
Outputs:
- block_out: bfloat16 [128, 65536], P('ch', 'vox')
- grad_features: float32 [128, 262144], P('ch', 'vox')
- grad_conv: float32 [27, 128, 128], P(None, None, 'ch')
- grad_qkv: float32 [3, 128, 128], P(None, None, 'ch')
- grad_out: float32 [128, 128], P('ch')
Inputs may be any that keep to these rules, and one draw needn't show every extreme that they name: Cell g = d * 4096 + x * 16 * 16 + y * 16 + z sits at grid point (d * 16 + x, y, z) of a grid of 16 * 64 by 16 by 16 points. neighbours[k, g], k = 9 (dx + 1) + 3 (dy + 1) + (dz + 1), is -1 unless both cells are occupied and the point at offset (dx, dy, dz) is in the grid; else it is (x + dx + 1) * 16 * 16 + (y + dy) * 16 + (z + dz), that cell's index in device d's cells extended by 256 cells on each side. A cell is occupied exactly when its send_slot is not -1; the relation is symmetric between offsets k and 26 - k. `send_slot`: an occupied cell of device s holds d * 16 + j: it is row j of the rows that device s sends to the patch of device d. On each device every value appears at most once and the rows to one patch take slots 0 upward. Every device fills all 16 slots of some patch, and some patch receives 16 rows from every device. `recv_slot`: slot i of device d holds s * 16 + j for row j that device s sends to d, or -1 for an empty slot; every row sent to d appears exactly once.
All inputs are finite; a program needn't handle non-finite values.
Results may differ from a plain program's by a relative error of at most 0.028.
The roundings to bfloat16 on the way count: a program that leaves them out, or rounds other values in their place, can miss the bound.
Values may be sent and summed in bfloat16 or wider, within the bound.
A program may use at most 64 MiB of HBM per device.

v0:
```python
import jax
import jax.numpy as jnp
from jax import lax
from jax.sharding import Mesh
from jax.sharding import PartitionSpec as P

C = 128
HEADS = 8
PATCH = 1024
FY = 16
FZ = 16
VOX = ("vox_0", "vox_1", "vox_2")


def extended(shard, sides, width):
    for axis, dim in sides:
        size, length = (lax.axis_size(axis), shard.shape[dim])
        up = [(i, (i + 1) % size) for i in range(size - 1)]
        down = [(j, i) for i, j in up]
        last = lax.slice_in_dim(shard, length - width, length, axis=dim)
        leading = lax.slice_in_dim(shard, 0, width, axis=dim)
        before = lax.ppermute(last, axis, up)
        after = lax.ppermute(leading, axis, down)
        shard = jnp.concatenate([before, shard, after], axis=dim)
    return shard


def joined_along(pieces, dim):
    pieces = jnp.moveaxis(pieces, 0, dim)
    shape = pieces.shape
    return pieces.reshape(*shape[:dim], shape[dim] * shape[dim + 1], *shape[dim + 2 :])


def from_everyone(shard, axis):
    copies = jnp.broadcast_to(shard, (lax.axis_size(axis), *shard.shape))
    return lax.all_to_all(copies, axis, split_axis=0, concat_axis=0, tiled=True)


def gather_directly(shard, axis, dim):
    return joined_along(from_everyone(shard, axis), dim)


def sent_together(arrays, axis, dim, along):
    widths = [a.shape[along] for a in arrays]
    both = jnp.concatenate(arrays, axis=along)
    filled = lax.all_gather(both, axis, axis=dim, tiled=True)
    return tuple(jnp.split(filled, [sum(widths[:k]) for k in range(1, len(widths))], axis=along))


def split_up(shard, dim, size):
    before, after = (shard.shape[:dim], shard.shape[dim + 1 :])
    return jnp.moveaxis(shard.reshape(*before, size, -1, *after), dim, 0)


def sent_and_summed(shard, axis, dim):
    size = lax.axis_size(axis)
    pieces = lax.all_to_all(split_up(shard, dim, size), axis, 0, 0, tiled=True)
    return jnp.sum(pieces, axis=0)


def sum_by_axis(shard, axes, dim):
    far, near = axes
    own = sent_and_summed(split_up(shard, dim, lax.axis_size(far)), near, dim + 1)
    return jnp.sum(lax.all_to_all(own, far, 0, 0, tiled=True), axis=0)


def rows_for(lines, size):
    spare = -lines.shape[0] % size
    if not spare:
        return lines
    return jnp.concatenate([lines, jnp.zeros((spare, *lines.shape[1:]), lines.dtype)])


def gather_axes(shard, axes, dim):
    far, near = axes
    leading = from_everyone(shard, far)
    pieces = jnp.swapaxes(from_everyone(leading, near), 0, 1)
    return joined_along(pieces.reshape(-1, *shard.shape), dim)


def nested_sum(shard, axes):
    own = sum_by_axis(rows_for(shard, lax.axis_size(axes[0]) * lax.axis_size(axes[1])), axes, 0)
    whole = gather_axes(own, axes, 0)
    return whole[: len(shard)].reshape(shard.shape)


def in_one(arrays, axis):
    line, at, done = (jnp.concatenate([a.reshape(-1) for a in arrays]), 0, [])
    running = nested_sum(line, axis)
    for a in arrays:
        done.append(running[at : at + a.size].reshape(a.shape))
        at += a.size
    return tuple(done)


def rims(field):
    return extended(field, ((VOX, 1),), FY * FZ)


def channels(field):
    return lax.all_gather(field, "ch", axis=0, tiled=True)


def regroup(field, out_slot, in_slot):
    slots_buffer = (
        jnp.zeros((field.shape[0], PATCH), field.dtype)
        .at[:, jnp.where(out_slot >= 0, out_slot, PATCH)]
        .set(field, mode="drop")
    )
    arrived = lax.all_to_all(slots_buffer, VOX, split_axis=1, concat_axis=1, tiled=True)
    picked = jnp.take(arrived, jnp.maximum(in_slot, 0), axis=1)
    return jnp.where(in_slot[None, :] >= 0, picked, jnp.zeros((), field.dtype))


def tap_offsets():
    offsets = []
    for offset_x in (-1, 0, 1):
        for offset_y in (-1, 0, 1):
            for offset_z in (-1, 0, 1):
                offsets.append(offset_x * FY * FZ + offset_y * FZ + offset_z)
    return offsets


def pad_flat(halo_field):
    return jnp.pad(halo_field, ((0, 0), (FZ + 1, FZ + 1)))


def one_tap(padded, present, which, cell_count):
    start = FZ + 1 + FY * FZ + tap_offsets()[which]
    window = lax.slice_in_dim(padded, start, start + cell_count, axis=1)
    return jnp.where(present[which][None, :], window, jnp.zeros((), padded.dtype))


def stack_taps(halo_field, present, cell_count):
    padded = pad_flat(halo_field)
    return jnp.stack([one_tap(padded, present, which, cell_count) for which in range(27)], axis=1)


def attend(query_rows, key_rows, value_rows, live_mask, grad_attn):
    scale = (C // HEADS) ** (-0.5)
    logits = (
        jnp.einsum("hdq,hdk->hqk", query_rows, key_rows, preferred_element_type=jnp.float32) * scale
    )
    logits = jnp.where(live_mask[None, None, :], logits, -1e30)
    largest = jnp.max(logits, axis=-1, keepdims=True)
    exponents = jnp.exp(logits - largest)
    probs = (exponents / jnp.sum(exponents, axis=-1, keepdims=True)).astype(jnp.bfloat16)
    attended = jnp.einsum(
        "hqk,hdk->hdq", probs, value_rows, preferred_element_type=jnp.float32
    ).astype(jnp.bfloat16)
    grad_logits = jnp.einsum(
        "hdq,hdk->hqk", grad_attn, value_rows, preferred_element_type=jnp.float32
    )
    probs_f32 = probs.astype(jnp.float32)
    grad_scores = (
        probs_f32 * (grad_logits - jnp.sum(probs_f32 * grad_logits, axis=-1, keepdims=True)) * scale
    ).astype(jnp.bfloat16)
    grad_query = jnp.einsum(
        "hqk,hdk->hdq", grad_scores, key_rows, preferred_element_type=jnp.float32
    ).astype(jnp.bfloat16)
    grad_key = jnp.einsum(
        "hqk,hdq->hdk", grad_scores, query_rows, preferred_element_type=jnp.float32
    ).astype(jnp.bfloat16)
    grad_value = jnp.einsum(
        "hqk,hdq->hdk", probs, grad_attn, preferred_element_type=jnp.float32
    ).astype(jnp.bfloat16)
    return (attended, grad_query, grad_key, grad_value)


def body(
    features, conv_weight, qkv_weight, out_weight, cotangent, neighbours, send_slot, recv_slot
):
    local_rows, cell_count = features.shape
    ch_index = lax.axis_index("ch")
    present = neighbours >= 0
    contract_first = (((0,), (0,)), ((), ()))
    full_weight = gather_directly(conv_weight, "ch", 2)
    own_weight = lax.dynamic_slice_in_dim(full_weight, ch_index * local_rows, local_rows, 1)
    halo_full = rims(channels(features))
    halo_local = lax.dynamic_slice_in_dim(halo_full, ch_index * local_rows, local_rows, 0)
    stacked = stack_taps(halo_local, present, cell_count)
    padded_full = pad_flat(halo_full)
    conv_out = jnp.zeros((local_rows, cell_count), jnp.float32)
    for which in range(27):
        columns = one_tap(padded_full, present, which, cell_count)
        conv_out = conv_out + jnp.dot(
            own_weight[which], columns, preferred_element_type=jnp.float32
        )
    layer_one = (features.astype(jnp.float32) + conv_out).astype(jnp.bfloat16)
    grouped = regroup(layer_one, send_slot, recv_slot)
    live_mask = recv_slot >= 0
    whole = channels(grouped).astype(jnp.float32)
    col_mean = jnp.mean(whole, axis=0, keepdims=True)
    centred = whole - col_mean
    col_var = jnp.mean(centred * centred, axis=0, keepdims=True)
    inverse = lax.rsqrt(col_var + 1e-05)
    normal_f32 = centred * inverse
    normed = normal_f32.astype(jnp.bfloat16)
    projected = [
        lax.dot_general(
            qkv_weight[which], normed, contract_first, preferred_element_type=jnp.float32
        ).astype(jnp.bfloat16)
        for which in range(3)
    ]
    masked_cot = jnp.where(live_mask[None, :], cotangent, jnp.zeros((), jnp.bfloat16))
    cot_whole = channels(masked_cot)
    grad_attn = jnp.dot(out_weight, cot_whole, preferred_element_type=jnp.float32).astype(
        jnp.bfloat16
    )
    head_size = C // HEADS
    local_heads = local_rows // head_size

    def split_heads(array):
        return array.reshape(local_heads, head_size, PATCH)

    attended, grad_query, grad_key, grad_value = attend(
        split_heads(projected[0]),
        split_heads(projected[1]),
        split_heads(projected[2]),
        live_mask,
        split_heads(grad_attn),
    )
    attended = attended.reshape(local_rows, PATCH)
    grad_parts = [
        part_grad.reshape(local_rows, PATCH) for part_grad in (grad_query, grad_key, grad_value)
    ]
    attended_full, weight_full = sent_together((attended, out_weight), "ch", 0, 1)
    own_columns = lax.dynamic_slice_in_dim(weight_full, ch_index * local_rows, local_rows, 1)
    mixed_out = lax.dot_general(
        own_columns, attended_full, contract_first, preferred_element_type=jnp.float32
    )
    block_out = jnp.where(live_mask[None, :], grouped.astype(jnp.float32) + mixed_out, 0.0).astype(
        jnp.bfloat16
    )
    grad_out_local = lax.dot_general(
        attended, cot_whole, (((1,), (1,)), ((), ())), preferred_element_type=jnp.float32
    )
    grad_qkv_local = jnp.stack(
        [
            lax.dot_general(
                normed, part_grad, (((1,), (1,)), ((), ())), preferred_element_type=jnp.float32
            )
            for part_grad in grad_parts
        ]
    )
    grads_stacked = jnp.stack(grad_parts)
    weights_turned = jnp.transpose(qkv_weight, (0, 2, 1))
    grads_full, turned_full = sent_together((grads_stacked, weights_turned), "ch", 1, 2)
    full_sum = lax.dot_general(
        turned_full[0], grads_full[0], contract_first, preferred_element_type=jnp.float32
    )
    full_sum = full_sum + lax.dot_general(
        turned_full[1], grads_full[1], contract_first, preferred_element_type=jnp.float32
    )
    full_sum = full_sum + lax.dot_general(
        turned_full[2], grads_full[2], contract_first, preferred_element_type=jnp.float32
    )
    grad_norm_f32 = full_sum.astype(jnp.bfloat16).astype(jnp.float32)
    grad_ln = inverse * (
        grad_norm_f32
        - jnp.mean(grad_norm_f32, axis=0, keepdims=True)
        - normal_f32 * jnp.mean(grad_norm_f32 * normal_f32, axis=0, keepdims=True)
    )
    own_ln = lax.dynamic_slice_in_dim(grad_ln, ch_index * local_rows, local_rows, 0)
    grad_grouped = jnp.where(
        live_mask[None, :], masked_cot.astype(jnp.float32) + own_ln, 0.0
    ).astype(jnp.bfloat16)
    grad_layer = regroup(grad_grouped, recv_slot, send_slot)
    layer_whole = channels(grad_layer)
    grad_conv_local = jnp.einsum(
        "ov,ckv->koc", layer_whole, stacked, preferred_element_type=jnp.float32
    )
    grad_padded = pad_flat(rims(layer_whole))
    grad_input = jnp.zeros((local_rows, cell_count), jnp.float32)
    for which in range(27):
        columns = one_tap(grad_padded, present, 26 - which, cell_count)
        grad_input = grad_input + lax.dot_general(
            conv_weight[which], columns, contract_first, preferred_element_type=jnp.float32
        )
    grad_features = grad_layer.astype(jnp.float32) + grad_input
    grad_conv, grad_qkv, grad_out = in_one(
        (grad_conv_local, grad_qkv_local, grad_out_local), (("vox_0", "vox_1"), "vox_2")
    )
    return (block_out, grad_features, grad_conv, grad_qkv, grad_out)


def solution(mesh):
    torus = Mesh(mesh.devices.reshape(8, 4, 2, mesh.shape["ch"]), ("vox_0", "vox_1", "vox_2", "ch"))
    placed = (
        P("ch", VOX),
        P(None, None, "ch"),
        P(None, None, "ch"),
        P("ch", None),
        P("ch", VOX),
        P(None, VOX),
        P(VOX),
        P(VOX),
    )
    return jax.shard_map(
        body,
        mesh=torus,
        in_specs=placed,
        out_specs=(
            P("ch", VOX),
            P("ch", VOX),
            P(None, None, "ch"),
            P(None, None, "ch"),
            P("ch", None),
        ),
        check_vma=False,
    )
```

profile of v0, /device:TPU:1, one launch (start us, length us, event | category | flops | bytes accessed | tf_op | source)
XLA Modules:
  0.0 360.5 jit_solution(15669462105090644)
XLA Ops:
  7.9 2.0 broadcast_in_dim.606
  9.9 7.8 %all-to-all-start = ((bf16[8,27,128,16]{2,3,1,0:T(8,128)(2,1)}), bf16[8,27,128,16]{2,3,1,0:T(8,128)(2,1)S(1)}, u32[]{:S(2)}, u32[]{:S(2)}) async-start(bf16[8,27,128,16]{2,3,1,0:T(8,128)(2,1)} %broadcast_in_dim.606), calls=%async_computation | async-start | bytes 1769472 | tf_op jit(solution)/shard_map/all_to_all | solution.py:36
  17.9 39.2 %all_gather.21 = bf16[128,1024]{1,0:T(8,128)(2,1)S(1)} all-gather(bf16[16,1024]{1,0:T(8,128)(2,1)S(1)} %broadcast_select_fusion), channel_id=1, replica_groups=mesh['vox_0'=8,'vox_1'=4,'vox_2'=2,'ch'=8] {'ch'}, dimensions={0}, use_global_device_ids=true | all-gather | bytes 294912 | tf_op jit(solution)/shard_map/all_gather | solution.py:101
  57.1 0.9 slice_reduce_fusion
  59.4 0.9 fusion.408
  60.3 10.0 %collective-permute-start = (bf16[128,256]{1,0:T(8,128)(2,1)S(1)}, bf16[128,256]{1,0:T(8,128)(2,1)S(1)}, u32[]{:S(2)}, u32[]{:S(2)}) collective-permute-start(bf16[128,256]{1,0:T(8,128)(2,1)S(1)} %get-tuple-element.59), channel_id=1, source_target_pairs={{0,8},{8,16},{16,24},{24,32},{32,40},{40,48},{48,56},{56,64},{64,7... | collective-permute-start | bytes 196616 | tf_op jit(solution)/shard_map/ppermute | solution.py:22
  70.9 2.1 collective-permute-start.1
  73.3 3.2 collective-permute-done.1
  91.6 10.8 %scatter_custom_fusion = bf16[16,1024]{0,1:T(8,128)(2,1)S(1)} fusion(s32[4096]{0:T(1024)S(1)} %get-tuple-element.68, bf16[4096,16]{1,0:T(8,128)(2,1)S(1)} %copy.46, bf16[]{:T(256)} %constant.24.clone.1), kind=kCustom, calls=%fused_computation.380 | custom fusion | bytes 32770 | tf_op jit(solution)/shard_map/scatter | solution.py:108
  102.4 0.8 reshape.224
  103.2 17.3 %all-to-all-start.1 = ((bf16[64,2,128]{2,1,0:T(2,128)(2,1)}), bf16[64,2,128]{2,1,0:T(2,128)(2,1)S(1)}, u32[]{:S(2)}, u32[]{:S(2)}) async-start(bf16[64,2,128]{2,1,0:T(2,128)(2,1)} %reshape.224), calls=%async_computation.1 | async-start | bytes 65536 | tf_op jit(solution)/shard_map/all_to_all | solution.py:110
  122.1 0.8 bitcast_dynamic-update-slice_fusion.5
  125.8 0.8 fusion.239
  127.3 0.8 fusion.235
  128.9 0.8 fusion.231
  131.8 0.8 fusion.223
  132.6 0.8 fusion.221
  134.9 0.8 fusion.215
  136.4 0.8 fusion.211
  139.6 3.2 gather_fusion
  142.9 18.9 %all_gather.19 = bf16[128,1024]{1,0:T(8,128)(2,1)S(1)} all-gather(bf16[16,1024]{1,0:T(8,128)(2,1)S(1)} %select_bitcast_fusion.1), channel_id=1, replica_groups=mesh['vox_0'=8,'vox_1'=4,'vox_2'=2,'ch'=8] {'ch'}, dimensions={0}, use_global_device_ids=true | all-gather | bytes 294912 | tf_op jit(solution)/shard_map/all_gather | solution.py:101
  162.5 0.8 fusion.36
  163.3 0.9 fusion.37
  164.2 1.6 fusion.33
  166.4 0.9 fusion.35
  168.4 21.0 %all_gather.22 = bf16[3,128,1152]{2,1,0:T(8,128)(2,1)S(1)} all-gather(bf16[3,16,1152]{2,1,0:T(8,128)(2,1)S(1)} %pad_maximum_fusion.1), channel_id=1, replica_groups=mesh['vox_0'=8,'vox_1'=4,'vox_2'=2,'ch'=8] {'ch'}, dimensions={1}, use_global_device_ids=true | all-gather | bytes 995328 | tf_op jit(solution)/shard_map/all_gather | solution.py:46
  190.4 3.4 scatter_custom_fusion.1
  193.8 0.8 reshape.226
  194.6 22.3 %all-to-all-start.2 = ((bf16[64,2,128]{2,1,0:T(2,128)(2,1)}), bf16[64,2,128]{2,1,0:T(2,128)(2,1)S(1)}, u32[]{:S(2)}, u32[]{:S(2)}) async-start(bf16[64,2,128]{2,1,0:T(2,128)(2,1)} %reshape.226), calls=%async_computation.2 | async-start | bytes 65536 | tf_op jit(solution)/shard_map/all_to_all | solution.py:110
  217.7 8.5 %all-to-all-done.2 = bf16[64,2,128]{2,1,0:T(2,128)(2,1)S(1)} async-done(((bf16[64,2,128]{2,1,0:T(2,128)(2,1)}), bf16[64,2,128]{2,1,0:T(2,128)(2,1)S(1)}, u32[]{:S(2)}, u32[]{:S(2)}) %all-to-all-start.2) | async-done | bytes 32800 | tf_op jit(solution)/shard_map/all_to_all | solution.py:110
  226.4 14.9 %gather_fusion.1 = bf16[4096,16]{1,0:T(8,128)(2,1)} fusion(bf16[16,1024]{0,1:T(8,128)(2,1)S(1)} %bitcast.390, s32[4096]{0:T(1024)S(1)} %get-tuple-element.67), kind=kCustom, calls=%fused_computation.1 | custom fusion | bytes 278528 | tf_op jit(solution)/shard_map/jit(_take)/gather | solution.py:111
  241.3 1.5 copy.50
  244.8 20.0 %all_gather.20 = bf16[128,1152]{1,0:T(8,128)(2,1)S(1)} all-gather(bf16[16,1152]{1,0:T(8,128)(2,1)S(1)} %pad_maximum_fusion.2), channel_id=1, replica_groups=mesh['vox_0'=8,'vox_1'=4,'vox_2'=2,'ch'=8] {'ch'}, dimensions={0}, use_global_device_ids=true | all-gather | bytes 331776 | tf_op jit(solution)/shard_map/all_gather | solution.py:46
  265.8 0.9 fusion.47
  266.7 7.3 %all-gather.5.cloned.1.call-done = bf16[128,4096]{1,0:T(8,128)(2,1)} async-done(((bf16[16,4096]{1,0:T(8,128)(2,1)}), bf16[128,4096]{1,0:T(8,128)(2,1)}) %all-gather.5.cloned.1.call-update) | async-done | bytes 1048592 | tf_op jit(solution)/shard_map/all_gather | solution.py:101
  273.9 0.9 fusion.407
  274.8 7.9 %collective-permute-start.2 = (bf16[128,256]{1,0:T(8,128)(2,1)S(1)}, bf16[128,256]{1,0:T(8,128)(2,1)S(1)}, u32[]{:S(2)}, u32[]{:S(2)}) collective-permute-start(bf16[128,256]{1,0:T(8,128)(2,1)S(1)} %get-tuple-element.53), channel_id=1, source_target_pairs={{0,8},{8,16},{16,24},{24,32},{32,40},{40,48},{48,56},{56,64},{64,7... | collective-permute-start | bytes 196616 | tf_op jit(solution)/shard_map/ppermute | solution.py:22
  282.7 1.9 collective-permute-start.3
  284.7 3.4 convolution_bitcast_fusion.10
  289.5 3.6 all_to_all.57
  293.8 11.7 %all-to-all-start.4 = ((f32[32,1,992]{2,1,0:T(1,128)}), f32[32,1,992]{2,1,0:T(1,128)S(1)}, u32[]{:S(2)}, u32[]{:S(2)}) async-start(f32[32,1,992]{2,1,0:T(1,128)} %all_to_all.45), calls=%async_computation.4 | async-start | bytes 262144 | tf_op jit(solution)/shard_map/all_to_all | solution.py:64
  321.3 9.3 %all-to-all-start.5 = ((f32[32,1,992]{2,1,0:T(1,128)}), f32[32,1,992]{2,1,0:T(1,128)S(1)}, u32[]{:S(2)}, u32[]{:S(2)}) async-start(f32[32,1,992]{2,1,0:T(1,128)} %broadcast_in_dim.700), calls=%async_computation.5 | async-start | bytes 262144 | tf_op jit(solution)/shard_map/all_to_all | solution.py:36
  330.7 1.0 fusion.1
  331.6 8.4 %all-to-all-done.5 = f32[32,1,992]{2,1,0:T(1,128)S(1)} async-done(((f32[32,1,992]{2,1,0:T(1,128)}), f32[32,1,992]{2,1,0:T(1,128)S(1)}, u32[]{:S(2)}, u32[]{:S(2)}) %all-to-all-start.5) | async-done | bytes 127008 | tf_op jit(solution)/shard_map/all_to_all | solution.py:36
  340.0 6.0 %all_to_all.58 = f32[2,32,992]{2,1,0:T(8,128)S(1)} all-to-all(f32[2,32,992]{2,1,0:T(8,128)S(1)} %broadcast_in_dim.701), channel_id=1, replica_groups=mesh['vox_0'=8,'vox_1'=4,'vox_2'=2,'ch'=8] {'vox_2'}, dimensions={0} | all-to-all | bytes 507904 | tf_op jit(solution)/shard_map/all_to_all | solution.py:36
  346.2 1.0 slice.863
  347.2 1.4 slice.953
  349.4 2.7 copy.56
  (220 shorter events, 58.4 us)
Async XLA Ops:
  7.2 52.2 %all-gather.3.cloned.1.call-start = ((), (), s32[]{:S(2)}) async-start(), calls=%async_computation.7 | async-start | bytes 1179648 | tf_op jit(solution)/shard_map/all_gather | solution.py:101
  7.9 9.8 %copy-start.33 = (s32[1024]{0:T(1024)S(1)}, s32[1024]{0:T(1024)}, u32[]{:S(2)}) copy-start(s32[1024]{0:T(1024)} %param.15) | copy-start | bytes 12292
  7.9 9.8 %copy-start.5 = (bf16[16,1024]{1,0:T(8,128)(2,1)S(1)}, bf16[16,1024]{1,0:T(8,128)(2,1)}, u32[]{:S(2)}) copy-start(bf16[16,1024]{1,0:T(8,128)(2,1)} %param.12) | copy-start | bytes 98308
  7.9 9.8 %copy-start.3 = (s32[27,4096]{1,0:T(8,128)S(1)}, s32[27,4096]{1,0:T(8,128)}, u32[]{:S(2)}) copy-start(s32[27,4096]{1,0:T(8,128)} %param.13) | copy-start | bytes 1327108
  9.9 48.6 %copy-start.8 = (s32[4096]{0:T(1024)S(1)}, s32[4096]{0:T(1024)}, u32[]{:S(2)}) copy-start(s32[4096]{0:T(1024)} %param.14) | copy-start | bytes 49156
  9.9 49.2 %copy-start.13 = (bf16[16,128]{1,0:T(8,128)(2,1)S(1)}, bf16[16,128]{1,0:T(8,128)(2,1)}, u32[]{:S(2)}) copy-start(bf16[16,128]{1,0:T(8,128)(2,1)} %param.11) | copy-start | bytes 12292
  9.9 60.7 %all-to-all-start = ((bf16[8,27,128,16]{2,3,1,0:T(8,128)(2,1)}), bf16[8,27,128,16]{2,3,1,0:T(8,128)(2,1)S(1)}, u32[]{:S(2)}, u32[]{:S(2)}) async-start(bf16[8,27,128,16]{2,3,1,0:T(8,128)(2,1)} %broadcast_in_dim.606), calls=%async_computation | async-start | bytes 1769472 | tf_op jit(solution)/shard_map/all_to_all | solution.py:36
  57.9 73.9 %copy-start.11 = (pred[4096]{0:T(1024)(128)(4,1)}, pred[4096]{0:T(1024)(128)(4,1)S(1)}, u32[]{:S(2)}) copy-start(pred[4096]{0:T(1024)(128)(4,1)S(1)} %get-tuple-element.33) | copy-start | bytes 12292
  58.0 74.6 %copy-start.9 = (pred[4096]{0:T(1024)(128)(4,1)}, pred[4096]{0:T(1024)(128)(4,1)S(1)}, u32[]{:S(2)}) copy-start(pred[4096]{0:T(1024)(128)(4,1)S(1)} %get-tuple-element.32) | copy-start | bytes 12292
  60.2 12.9 %copy-start.2 = (bf16[128,4096]{1,0:T(8,128)(2,1)S(1)}, bf16[128,4096]{1,0:T(8,128)(2,1)}, u32[]{:S(2)}) copy-start(bf16[128,4096]{1,0:T(8,128)(2,1)} %all-gather.3.cloned.1.call-done) | copy-start | bytes 3145732
  60.3 12.8 %collective-permute-start = (bf16[128,256]{1,0:T(8,128)(2,1)S(1)}, bf16[128,256]{1,0:T(8,128)(2,1)S(1)}, u32[]{:S(2)}, u32[]{:S(2)}) collective-permute-start(bf16[128,256]{1,0:T(8,128)(2,1)S(1)} %get-tuple-element.59), channel_id=1, source_target_pairs={{0,8},{8,16},{16,24},{24,32},{32,40},{40,48},{48,56},{56,64},{64,7... | collective-permute-start | bytes 196616 | tf_op jit(solution)/shard_map/ppermute | solution.py:22
  70.6 49.9 %copy-start.15 = (pred[4096]{0:T(1024)(128)(4,1)}, pred[4096]{0:T(1024)(128)(4,1)S(1)}, u32[]{:S(2)}) copy-start(pred[4096]{0:T(1024)(128)(4,1)S(1)} %get-tuple-element.48) | copy-start | bytes 12292
  70.6 50.7 %copy-start.17 = (pred[4096]{0:T(1024)(128)(4,1)}, pred[4096]{0:T(1024)(128)(4,1)S(1)}, u32[]{:S(2)}) copy-start(pred[4096]{0:T(1024)(128)(4,1)S(1)} %get-tuple-element.47) | copy-start | bytes 12292
  70.6 51.4 %copy-start.19 = (pred[4096]{0:T(1024)(128)(4,1)}, pred[4096]{0:T(1024)(128)(4,1)S(1)}, u32[]{:S(2)}) copy-start(pred[4096]{0:T(1024)(128)(4,1)S(1)} %get-tuple-element.46) | copy-start | bytes 12292
  70.6 52.2 %copy-start.21 = (pred[4096]{0:T(1024)(128)(4,1)}, pred[4096]{0:T(1024)(128)(4,1)S(1)}, u32[]{:S(2)}) copy-start(pred[4096]{0:T(1024)(128)(4,1)S(1)} %get-tuple-element.45) | copy-start | bytes 12292
  70.6 53.0 %copy-start.23 = (pred[4096]{0:T(1024)(128)(4,1)}, pred[4096]{0:T(1024)(128)(4,1)S(1)}, u32[]{:S(2)}) copy-start(pred[4096]{0:T(1024)(128)(4,1)S(1)} %get-tuple-element.44) | copy-start | bytes 12292
  70.7 53.6 %copy-start.25 = (pred[4096]{0:T(1024)(128)(4,1)}, pred[4096]{0:T(1024)(128)(4,1)S(1)}, u32[]{:S(2)}) copy-start(pred[4096]{0:T(1024)(128)(4,1)S(1)} %get-tuple-element.43) | copy-start | bytes 12292
  70.7 54.4 %copy-start.27 = (pred[4096]{0:T(1024)(128)(4,1)}, pred[4096]{0:T(1024)(128)(4,1)S(1)}, u32[]{:S(2)}) copy-start(pred[4096]{0:T(1024)(128)(4,1)S(1)} %get-tuple-element.42) | copy-start | bytes 12292
  70.7 55.1 %copy-start.29 = (pred[4096]{0:T(1024)(128)(4,1)}, pred[4096]{0:T(1024)(128)(4,1)S(1)}, u32[]{:S(2)}) copy-start(pred[4096]{0:T(1024)(128)(4,1)S(1)} %get-tuple-element.41) | copy-start | bytes 12292
  70.9 5.6 %collective-permute-start.1 = (bf16[128,256]{1,0:T(8,128)(2,1)S(1)}, bf16[128,256]{1,0:T(8,128)(2,1)S(1)}, u32[]{:S(2)}, u32[]{:S(2)}) collective-permute-start(bf16[128,256]{1,0:T(8,128)(2,1)S(1)} %get-tuple-element.58), channel_id=1, source_target_pairs={{8,0},{16,8},{24,16},{32,24},{40,32},{48,40},{56,48},{64,56},{72,6... | collective-permute-start | bytes 196616 | tf_op jit(solution)/shard_map/ppermute | solution.py:23
  89.4 0.9 copy-start.6
  103.2 36.2 %all-to-all-start.1 = ((bf16[64,2,128]{2,1,0:T(2,128)(2,1)}), bf16[64,2,128]{2,1,0:T(2,128)(2,1)S(1)}, u32[]{:S(2)}, u32[]{:S(2)}) async-start(bf16[64,2,128]{2,1,0:T(2,128)(2,1)} %reshape.224), calls=%async_computation.1 | async-start | bytes 65536 | tf_op jit(solution)/shard_map/all_to_all | solution.py:110
  137.8 24.1 %copy-start.34 = (bf16[3,128,16]{1,2,0:T(8,128)(2,1)S(1)}, bf16[3,128,16]{1,2,0:T(8,128)(2,1)}, u32[]{:S(2)}) copy-start(bf16[3,128,16]{1,2,0:T(8,128)(2,1)} %param.10) | copy-start | bytes 36868
  194.6 31.6 %all-to-all-start.2 = ((bf16[64,2,128]{2,1,0:T(2,128)(2,1)}), bf16[64,2,128]{2,1,0:T(2,128)(2,1)S(1)}, u32[]{:S(2)}, u32[]{:S(2)}) async-start(bf16[64,2,128]{2,1,0:T(2,128)(2,1)} %reshape.226), calls=%async_computation.2 | async-start | bytes 65536 | tf_op jit(solution)/shard_map/all_to_all | solution.py:110
  216.9 57.1 %all-gather.5.cloned.1.call-start = ((), (), s32[]{:S(2)}) async-start(), calls=%async_computation.8 | async-start | bytes 1179648 | tf_op jit(solution)/shard_map/all_gather | solution.py:101
  226.4 16.4 %copy-start.31 = (pred[4096]{0:T(1024)(128)(4,1)S(1)}, pred[4096]{0:T(1024)(128)(4,1)}, u32[]{:S(2)}) copy-start(pred[4096]{0:T(1024)(128)(4,1)} %get-tuple-element.65) | copy-start | bytes 12292
  226.4 16.4 %copy-start.32 = (pred[4096]{0:T(1024)(128)(4,1)S(1)}, pred[4096]{0:T(1024)(128)(4,1)}, u32[]{:S(2)}) copy-start(pred[4096]{0:T(1024)(128)(4,1)} %get-tuple-element.66) | copy-start | bytes 12292
  243.6 1.2 copy-start.14
  274.8 31.0 %collective-permute-start.2 = (bf16[128,256]{1,0:T(8,128)(2,1)S(1)}, bf16[128,256]{1,0:T(8,128)(2,1)S(1)}, u32[]{:S(2)}, u32[]{:S(2)}) collective-permute-start(bf16[128,256]{1,0:T(8,128)(2,1)S(1)} %get-tuple-element.53), channel_id=1, source_target_pairs={{0,8},{8,16},{16,24},{24,32},{32,40},{40,48},{48,56},{56,64},{64,7... | collective-permute-start | bytes 196616 | tf_op jit(solution)/shard_map/ppermute | solution.py:22
  282.7 23.2 %collective-permute-start.3 = (bf16[128,256]{1,0:T(8,128)(2,1)S(1)}, bf16[128,256]{1,0:T(8,128)(2,1)S(1)}, u32[]{:S(2)}, u32[]{:S(2)}) collective-permute-start(bf16[128,256]{1,0:T(8,128)(2,1)S(1)} %get-tuple-element.54), channel_id=1, source_target_pairs={{8,0},{16,8},{24,16},{32,24},{40,32},{48,40},{56,48},{64,56},{72,6... | collective-permute-start | bytes 196616 | tf_op jit(solution)/shard_map/ppermute | solution.py:23
  289.1 16.4 %copy-start = (bf16[128,4096]{1,0:T(8,128)(2,1)S(1)}, bf16[128,4096]{1,0:T(8,128)(2,1)}, u32[]{:S(2)}) copy-start(bf16[128,4096]{1,0:T(8,128)(2,1)} %all-gather.5.cloned.1.call-done) | copy-start | bytes 3145732
  289.1 16.4 %copy-start.7 = (bf16[27,128,16]{1,2,0:T(8,128)(2,1)S(1)}, bf16[27,128,16]{1,2,0:T(8,128)(2,1)}, u32[]{:S(2)}) copy-start(bf16[27,128,16]{1,2,0:T(8,128)(2,1)} %param.9) | copy-start | bytes 331780
  293.8 26.7 %all-to-all-start.4 = ((f32[32,1,992]{2,1,0:T(1,128)}), f32[32,1,992]{2,1,0:T(1,128)S(1)}, u32[]{:S(2)}, u32[]{:S(2)}) async-start(f32[32,1,992]{2,1,0:T(1,128)} %all_to_all.45), calls=%async_computation.4 | async-start | bytes 262144 | tf_op jit(solution)/shard_map/all_to_all | solution.py:64
  306.0 0.7 copy-start.12
  306.6 0.7 copy-start.10
  315.2 0.7 copy-start.30
  315.9 0.7 copy-start.28
  316.6 0.7 copy-start.26
  317.3 0.7 copy-start.24
  318.0 0.7 copy-start.22
  318.6 0.7 copy-start.20
  319.3 0.7 copy-start.18
  320.0 10.6 %copy-start.4 = (bf16[16,4096]{1,0:T(8,128)(2,1)S(1)}, bf16[16,4096]{1,0:T(8,128)(2,1)}, u32[]{:S(2)}) copy-start(bf16[16,4096]{1,0:T(8,128)(2,1)} %select_bitcast_fusion) | copy-start | bytes 393220
  320.0 10.7 %copy-start.16 = (pred[4096]{0:T(1024)(128)(4,1)S(1)}, pred[4096]{0:T(1024)(128)(4,1)}, u32[]{:S(2)}) copy-start(pred[4096]{0:T(1024)(128)(4,1)} %copy-done.15) | copy-start | bytes 12292
  321.3 18.7 %all-to-all-start.5 = ((f32[32,1,992]{2,1,0:T(1,128)}), f32[32,1,992]{2,1,0:T(1,128)S(1)}, u32[]{:S(2)}, u32[]{:S(2)}) async-start(f32[32,1,992]{2,1,0:T(1,128)} %broadcast_in_dim.700), calls=%async_computation.5 | async-start | bytes 262144 | tf_op jit(solution)/shard_map/all_to_all | solution.py:36
  347.2 1.9 copy-start.1
  349.1 3.0 slice-start
Sparse Core Ops, SparseCore 0:
  10.1 47.0 all-gather.2
  243.7 30.2 all-gather.4
where the time goes:
time: 364 us; the launch traced here: 360 us
  blocking collectives  109 us (30%)
  starting transfers between devices  90.4 us (25%)
  local copies, waits for them, and re-layouts  55.2 us (15%)
  matrix products  38.2 us (10%)
  waiting for transfers between devices  28.1 us (8%)
  other arithmetic  25 us (7%)
  between operations  15.1 us (4%)
    all_gather x2, blocking collectives, channels(): return lax.all_gather(field, 'ch', axis=0, tiled=True)  58.1 us
    all_gather x2, blocking collectives, sent_together(): filled = lax.all_gather(both, axis, axis=dim, tiled=True)  41 us
    all_to_all x2, starting transfers between devices, regroup(): lax.all_to_all(slots_buffer, VOX, split_axis=1, concat_axis=1, tiled=True)  39.6 us
    gather x4, local copies, waits for them, and re-layouts, regroup(): picked = jnp.take(arrived, jnp.maximum(in_slot, 0), axis=1)  19.7 us
    unnamed x26, other arithmetic  19.5 us
    ppermute x2, starting transfers between devices, extended(): before = lax.ppermute(last, axis, up)  17.9 us
    all_to_all x2, starting transfers between devices, from_everyone(): return lax.all_to_all(copies, axis, split_axis=0, concat_axis=0, tiled=True)  17.1 us
    scatter x2, local copies, waits for them, and re-layouts, regroup(): slots_buffer = jnp.zeros((field.shape[0], PATCH), field.dtype).at[:, jnp....  14.2 us
  transfers between devices with their start and end apart: 11, of which 4 were waited for; matrix products, arithmetic and copies ran while one was open for 13% of the time, Pallas kernels for 0%

commit v1 on v0

v1 whole, which is shorter than its diff:
```python
import jax
import jax.numpy as jnp
from jax import lax
from jax.experimental import pallas as pl
from jax.experimental.pallas import tpu as pltpu
from jax.sharding import Mesh
from jax.sharding import PartitionSpec as P

MESH = pl.DeviceIdType.MESH
VOX = ("vox_0", "vox_1", "vox_2")
BF = jnp.bfloat16
F32 = jnp.float32
CELLS = 4096
LAYER = 256
EXT = CELLS + 2 * LAYER
SLOTS = 1024
ORDER = (4, 3, 5, 2, 6, 1, 7)


def nn(a, b):
    return jnp.dot(a, b, preferred_element_type=F32)


def nt(a, b):
    return lax.dot_general(a, b, (((1,), (1,)), ((), ())), preferred_element_type=F32)


def tn(a, b):
    return lax.dot_general(a, b, (((0,), (0,)), ((), ())), preferred_element_type=F32)


def lanes(shape):
    return lax.broadcasted_iota(jnp.int32, shape, 1)


def swap_blocks(tiles):
    flat = tiles.reshape(128, 128)
    turned = [flat if s == 0 else pltpu.roll(flat, s * 16, 1) for s in range(8)]
    block = lanes((16, 128)) // 16
    out = []
    for j in range(8):
        tile = turned[(0 - j) % 8][0:16]
        for i in range(1, 8):
            tile = jnp.where(block == i, turned[(i - j) % 8][i * 16 : i * 16 + 16], tile)
        out.append(tile)
    return out


def in_layer(width, dy, dz):
    cell = lanes((16, width))
    row = (cell // 16) % 16 + dy
    col = cell % 16 + dz
    return (row >= 0) & (row < 16) & (col >= 0) & (col < 16)


def whole_kernel(
    f_ref, ss_ref, rs_ref, cot_ref, wb_ref, w2_ref, ow_ref,
    bo_ref, gf_ref, vv_ref,
    onehot, pick, fx, hx, hl, fm, wt, aw, w9, s9, layer, s1, a1, t1, a2, gw, cw, mine2, ww,
    kvt, qg, pk, acc, big, bsl, xs, ys, u1, c2, v1, d1, glw, gx, hf, hl2, hg,
    vs, e0, e1s, e2, f0, fz, f1, vg,
    ring_s, ring_r, ex_s, ex_r, halo_s, halo_r,
):
    z = lax.axis_index("vox_0")
    xc = lax.axis_index("vox_1") * 2 + lax.axis_index("vox_2")
    y = lax.axis_index("ch")
    d = z * 8 + xc

    def to_y(p):
        return {"ch": p}

    def to_z(p):
        return {"vox_0": p}

    def to_xc(p):
        return {"vox_1": p // 2, "vox_2": lax.rem(p, 2)}

    def to_d(p):
        return {"vox_0": p // 8, "vox_1": lax.rem(p, 8) // 2, "vox_2": lax.rem(p, 2)}

    after, before = lax.rem(d + 1, 64), lax.rem(d + 63, 64)

    barrier = pltpu.get_barrier_semaphore()
    for r in range(1, 8):
        for me, where in ((y, to_y), (z, to_z), (xc, to_xc)):
            pl.semaphore_signal(
                barrier, inc=1, device_id=where(lax.rem(me + r, 8)), device_id_type=MESH
            )
    for p in (after, before):
        pl.semaphore_signal(barrier, inc=1, device_id=to_d(p), device_id_type=MESH)

    sent = []

    def send(src, dst, s_sem, r_sem, where):
        copy = pltpu.make_async_remote_copy(
            src_ref=src, dst_ref=dst, send_sem=s_sem, recv_sem=r_sem,
            device_id=where, device_id_type=MESH,
        )
        copy.start()
        sent.append(copy)
        return copy

    def exchange(phase, me, where, src_of, dst):
        copies = []
        for r in ORDER:
            p = lax.rem(me + r, 8)
            copies.append(
                send(src_of(p), dst, ex_s.at[phase, r], ex_r.at[phase, r], where(p))
            )
        return copies

    def arrive(copies):
        for copy in copies:
            copy.wait_recv()

    def rows16(b):
        return pl.ds(pl.multiple_of(b * 16, 16), 16)

    def tile(b):
        return pl.ds(pl.multiple_of(b * 128, 128), 128)

    mine = rows16(y)
    ss = ss_ref[...]
    occupied = ss >= 0
    live = rs_ref[...] >= 0

    own = jnp.where(occupied, f_ref[...].astype(F32), 0.0).astype(BF)
    fm[...] = own
    fx[mine, LAYER : LAYER + CELLS] = own
    weights = jnp.concatenate([wb_ref[...].astype(F32), jnp.zeros((80, 128), F32)], axis=0)
    for t in range(4):
        wt[:, t * 128 : t * 128 + 128] = weights[t * 128 : t * 128 + 128, :].T.astype(BF)
    cw[mine, :] = jnp.where(live, cot_ref[...].astype(F32), 0.0).astype(BF)
    mine2[0:48, :] = w2_ref[...]
    mine2[48:64, :] = ow_ref[...]
    ww[y] = mine2[...]
    aw[y] = wt[mine, :]

    pl.semaphore_wait(barrier, 23)

    halo = [
        send(fm.at[:, CELLS - LAYER : CELLS], hl.at[0], halo_s.at[0], halo_r.at[0], to_d(after)),
        send(fm.at[:, 0:LAYER], hl.at[1], halo_s.at[1], halo_r.at[1], to_d(before)),
    ]

    def onehot_piece(piece):
        def step(i, carry):
            at = pl.multiple_of(piece * 64 + i * 16, 16)
            ids = lax.broadcasted_iota(jnp.int32, (16, CELLS), 0) + at
            onehot[pl.ds(at, 16), :] = jnp.where(ids == ss, 1.0, 0.0).astype(BF)
            return carry

        lax.fori_loop(0, 4, step, 0)

    source = rs_ref[...]
    route = (source >> 4) & 7
    spot = jnp.where(live, route * 128 + ((source >> 7) & 7) * 16 + (source & 15), -1)

    def pick_piece(piece):
        def step(i, carry):
            at = pl.multiple_of(piece * 256 + i * 16, 16)
            ids = lax.broadcasted_iota(jnp.int32, (16, SLOTS), 0) + at
            pick[pl.ds(at, 16), :] = jnp.where(ids == spot, 1.0, 0.0).astype(BF)
            return carry

        lax.fori_loop(0, 16, step, 0)

    work = [lambda i=i: onehot_piece(i) for i in range(16)]
    work += [lambda i=i: pick_piece(i) for i in range(4)]

    def chunk_of(c):
        if c < 4:
            return lambda b: fx.at[rows16(b), LAYER + c * 1024 : LAYER + c * 1024 + 1024]
        return lambda b: hx.at[rows16(b), :]

    chunks = [chunk_of(c) for c in range(5)]
    hops = ((4, 4, 3, 3, 4), (3, 3, 4, 4, 3))
    ring = {}
    for s in range(4):
        for c in range(5):
            if s == 0 and c == 4:
                arrive(halo)
                left = jnp.where(d == 0, 0.0, hl[0].astype(F32)).astype(BF)
                right = jnp.where(d == 63, 0.0, hl[1].astype(F32)).astype(BF)
                hx[mine, 0:LAYER] = left
                hx[mine, LAYER : 2 * LAYER] = right
            if s > 0 and work:
                work.pop(0)()
            for way in range(2):
                if s >= hops[way][c]:
                    continue
                if s > 0:
                    ring[way, s - 1, c].wait_recv()
                block = lax.rem(y + 8 - s, 8) if way == 0 else lax.rem(y + s, 8)
                to = lax.rem(y + 1, 8) if way == 0 else lax.rem(y + 7, 8)
                ring[way, s, c] = send(
                    chunks[c](block), chunks[c](block),
                    ring_s.at[way, s, c], ring_r.at[way, s, c], to_y(to),
                )
        if s == 0:
            got_aw = exchange(0, y, to_y, lambda p: wt.at[rows16(p), :], aw.at[y])
    while work:
        work.pop(0)()
    for c in range(5):
        for way in range(2):
            ring[way, hops[way][c] - 1, c].wait_recv()
    got_ww = exchange(1, y, to_y, lambda p: mine2, ww.at[y])
    got_cw = exchange(2, y, to_y, lambda p: cw.at[mine, :], cw.at[mine, :])
    fx[:, 0:LAYER] = hx[:, 0:LAYER]
    fx[:, LAYER + CELLS : EXT] = hx[:, LAYER : 2 * LAYER]

    arrive(got_aw)
    for t in range(4):
        for k, part in enumerate(swap_blocks(aw[:, :, t * 128 : t * 128 + 128].astype(F32))):
            if t * 8 + k < 27:
                at = (t * 8 + k) * 16
                w9[at : at + 16, :] = part.astype(BF)

    taps = [(dy, dz) for dy in (-1, 0, 1) for dz in (-1, 0, 1)]

    def conv_step(i, carry):
        total = None
        for dx in range(3):
            field = fx[:, pl.ds(pl.multiple_of(i * 512 + dx * LAYER, LAYER), 512)]
            term = nn(w9[dx * 144 : dx * 144 + 144, :], field)
            total = term if total is None else total + term
        out = fm[:, pl.ds(pl.multiple_of(i * 512, 512), 512)].astype(F32)
        conv = jnp.zeros((16, 512), F32)
        for j, (dy, dz) in enumerate(taps):
            shift = -(dy * 16 + dz) % 512
            slab = total[j * 16 : j * 16 + 16]
            slab = pltpu.roll(slab, shift, 1) if shift else slab
            conv = conv + jnp.where(in_layer(512, dy, dz), slab, 0.0)
        layer[:, pl.ds(pl.multiple_of(i * 512, 512), 512)] = (out + conv).astype(BF)
        return carry

    lax.fori_loop(0, 8, conv_step, 0)

    def pack_step(i, carry):
        rows = nt(layer[...], onehot[pl.ds(pl.multiple_of(i * 256, 256), 256), :])
        s1[2 * i] = rows[:, 0:128].astype(BF)
        s1[2 * i + 1] = rows[:, 128:256].astype(BF)
        return carry

    lax.fori_loop(0, 4, pack_step, 0)
    a1[z] = s1[z]
    got = exchange(3, z, to_z, lambda p: s1.at[p], a1.at[z])

    def shifted_step(i, carry):
        at = pl.ds(pl.multiple_of(i * 512, 512), 512)
        x = fx[mine, at].astype(F32)
        for j, (dy, dz) in enumerate(taps):
            shift = -(dy * 16 + dz) % 512
            slab = pltpu.roll(x, shift, 1) if shift else x
            s9[j * 16 : j * 16 + 16, at] = jnp.where(in_layer(512, dy, dz), slab, 0.0).astype(BF)
        return carry

    lax.fori_loop(0, EXT // 512, shifted_step, 0)

    arrive(got)
    for j, part in enumerate(swap_blocks(a1[...].astype(F32))):
        t1[j] = part.astype(BF)
    a2[xc] = t1[xc]
    got = exchange(4, xc, to_xc, lambda p: t1.at[p], a2.at[xc])
    arrive(got)
    arrived = jnp.concatenate([a2[i] for i in range(8)], axis=1)
    gw[mine, :] = nn(arrived, pick[...]).astype(BF)
    got = exchange(5, y, to_y, lambda p: gw.at[mine, :], gw.at[mine, :])
    arrive(got_cw)
    arrive(got_ww)
    ga = nn(ow_ref[...], cw[...]).astype(BF)
    arrive(got)

    whole = gw[...].astype(F32)
    mean = jnp.mean(whole, axis=0, keepdims=True)
    centred = whole - mean
    var = jnp.mean(centred * centred, axis=0, keepdims=True)
    normed = (centred * lax.rsqrt(var + 1e-05)).astype(BF)
    big[...] = normed
    qkv = nn(w2_ref[...], normed).astype(BF)
    quarter = (qkv[0:16].astype(F32) * 0.25).astype(BF)
    row = lax.broadcasted_iota(jnp.int32, (16, SLOTS), 0)
    bias = jnp.where((row == 0) & (~live), -1e30, 0.0)
    stacked = jnp.concatenate(
        [
            qkv[16:32].astype(F32),
            bias,
            qkv[32:48].astype(F32),
            jnp.zeros((80, SLOTS), F32),
        ],
        axis=0,
    )
    for t in range(8):
        kvt[t * 128 : t * 128 + 128, :] = stacked[:, t * 128 : t * 128 + 128].T.astype(BF)
    ones = jnp.where(lax.broadcasted_iota(jnp.int32, (16, 128), 0) == 0, 1.0, 0.0).astype(BF)
    for t in range(8):
        cols = slice(t * 128, t * 128 + 128)
        left = jnp.concatenate([quarter[:, cols], ones, jnp.zeros((96, 128), BF)], axis=0)
        right = jnp.concatenate(
            [jnp.zeros((32, 128), BF), ga[:, cols], jnp.zeros((80, 128), BF)], axis=0
        )
        qg[t] = jnp.concatenate([left, right], axis=1)
    vk = jnp.concatenate([qkv[32:48], qkv[16:32]], axis=0)
    mixed_rows = []
    for t in range(8):
        cols = slice(t * 128, t * 128 + 128)
        zero = jnp.zeros((16, 128), BF)
        mixed_rows.append(
            jnp.concatenate(
                [
                    jnp.concatenate([zero, qkv[0:16, cols]], axis=1),
                    jnp.concatenate([ga[:, cols], zero], axis=1),
                ],
                axis=0,
            )
        )
    for t in range(8):
        bsl[t] = mixed_rows[t]
    acc[...] = jnp.zeros((32, SLOTS), F32)

    def attend_step(i, carry):
        both = nn(kvt[...], qg[i])
        logits, grad_logits = both[:, 0:128], both[:, 128:256]
        exponents = jnp.exp(logits - jnp.max(logits, axis=0, keepdims=True))
        total = jnp.sum(exponents, axis=0, keepdims=True)
        probs = (exponents * (1.0 / total)).astype(BF)
        wide = probs.astype(F32)
        inner = jnp.sum(wide * grad_logits, axis=0, keepdims=True)
        scores = (wide * (grad_logits - inner) * 0.25).astype(BF)
        pair = jnp.concatenate([probs, scores], axis=1)
        near = nn(vk, pair)
        at = tile(i)
        pk[0:16, at] = near[0:16, 0:128].astype(BF)
        pk[16:32, at] = near[16:32, 128:256].astype(BF)
        acc[...] += nt(bsl[i], pair)
        return carry

    lax.fori_loop(0, 8, attend_step, 0)
    pk[32:64, :] = acc[...].astype(BF)

    ys[y] = pk[:, tile(y)]
    got = exchange(6, y, to_y, lambda p: pk.at[:, tile(p)], ys.at[y])
    vs[432:480, :] = nt(pk[16:64, :], big[...])
    vs[480:496, :] = nt(pk[0:16, :], cw[...])
    vs[496:512, :] = jnp.zeros((16, 128), F32)
    own_slots = tile(y)
    part = gw[:, own_slots].astype(F32)
    mean = jnp.mean(part, axis=0, keepdims=True)
    centred = part - mean
    var = jnp.mean(centred * centred, axis=0, keepdims=True)
    inverse = lax.rsqrt(var + 1e-05)
    normal = centred * inverse
    cot = cw[:, own_slots].astype(F32)
    live_part = rs_ref[:, own_slots] >= 0
    arrive(got)
    mixed = tn(ww[:, 48:64, :].reshape(128, 128), ys[:, 0:16, :].reshape(128, 128))
    grad = None
    for i in range(3):
        term = tn(
            ww[:, i * 16 : i * 16 + 16, :].reshape(128, 128),
            ys[:, 16 + i * 16 : 32 + i * 16, :].reshape(128, 128),
        )
        grad = term if grad is None else grad + term
    grad = grad.astype(BF).astype(F32)
    grad_ln = inverse * (
        grad
        - jnp.mean(grad, axis=0, keepdims=True)
        - normal * jnp.mean(grad * normal, axis=0, keepdims=True)
    )
    back = jnp.where(live_part, cot + grad_ln, 0.0).astype(BF)
    block = jnp.where(live_part, part + mixed, 0.0).astype(BF)
    xs[:, 0:16, :] = back.reshape(8, 16, 128)
    xs[:, 16:32, :] = block.reshape(8, 16, 128)
    u1[y] = xs[y]
    got = exchange(7, y, to_y, lambda p: xs.at[p], u1.at[y])
    arrive(got)
    grad_grouped = jnp.concatenate([u1[i, 0:16] for i in range(8)], axis=1)
    spread = nt(grad_grouped, pick[...])
    for t in range(8):
        c2[t] = spread[:, t * 128 : t * 128 + 128].astype(BF)
    v1[xc] = c2[xc]
    got = exchange(8, xc, to_xc, lambda p: c2.at[p], v1.at[xc])
    bo_ref[...] = jnp.concatenate([u1[i, 16:32] for i in range(8)], axis=1)
    arrive(got)
    for j, piece in enumerate(swap_blocks(v1[...].astype(F32))):
        d1[j] = piece.astype(BF)
    e0[z] = d1[z]
    got = exchange(9, z, to_z, lambda p: d1.at[p], e0.at[z])
    arrive(got)
    slots = jnp.concatenate([e0[i] for i in range(8)], axis=1)
    glw[mine, :] = slots
    got = exchange(10, y, to_y, lambda p: glw.at[mine, :], glw.at[mine, :])
    hf[:, 0:LAYER] = nn(slots, onehot[:, 0:LAYER]).astype(BF)
    hf[:, LAYER : 2 * LAYER] = nn(slots, onehot[:, CELLS - LAYER : CELLS]).astype(BF)
    halo = [
        send(hf.at[:, LAYER : 2 * LAYER], hl2.at[0], halo_s.at[2], halo_r.at[2], to_d(after)),
        send(hf.at[:, 0:LAYER], hl2.at[1], halo_s.at[3], halo_r.at[3], to_d(before)),
    ]
    arrive(halo)
    hg[mine, 0:LAYER] = jnp.where(d == 0, 0.0, hl2[0].astype(F32)).astype(BF)
    hg[mine, LAYER : 2 * LAYER] = jnp.where(d == 63, 0.0, hl2[1].astype(F32)).astype(BF)
    got_halo = exchange(11, y, to_y, lambda p: hg.at[mine, :], hg.at[mine, :])
    arrive(got)

    def expand_step(i, carry):
        at = pl.multiple_of(i * 512, 512)
        gx[:, pl.ds(pl.multiple_of(at + LAYER, LAYER), 512)] = nn(
            glw[...], onehot[:, pl.ds(at, 512)]
        ).astype(BF)
        return carry

    lax.fori_loop(0, 8, expand_step, 0)

    for dx in range(3):
        vs[dx * 144 : dx * 144 + 144, :] = nt(
            s9[:, dx * LAYER : dx * LAYER + CELLS], gx[:, LAYER : LAYER + CELLS]
        )

    def rows64(b):
        return pl.ds(pl.multiple_of(b * 64, 64), 64)

    def rows8(b):
        return pl.ds(pl.multiple_of(b * 8, 8), 8)

    e1s[xc] = vs[rows64(xc), :]
    got = exchange(12, xc, to_xc, lambda p: vs.at[rows64(p), :], e1s.at[xc])

    arrive(got_halo)
    gx[:, 0:LAYER] = hg[:, 0:LAYER]
    gx[:, LAYER + CELLS : EXT] = hg[:, LAYER : 2 * LAYER]

    def input_step(i, carry):
        total = None
        for dx in range(3):
            field = gx[:, pl.ds(pl.multiple_of(i * 512 + (2 - dx) * LAYER, LAYER), 512)]
            term = nn(wb_ref[dx * 144 : dx * 144 + 144, :], field)
            total = term if total is None else total + term
        at = pl.ds(pl.multiple_of(i * 512, 512), 512)
        conv = jnp.zeros((16, 512), F32)
        for j, (dy, dz) in enumerate(taps):
            shift = (dy * 16 + dz) % 512
            slab = total[j * 16 : j * 16 + 16]
            slab = pltpu.roll(slab, shift, 1) if shift else slab
            conv = conv + jnp.where(in_layer(512, -dy, -dz), slab, 0.0)
        own_grad = gx[mine, pl.ds(pl.multiple_of(i * 512 + LAYER, LAYER), 512)].astype(F32)
        gf_ref[:, at] = own_grad + jnp.where(ss_ref[:, at] >= 0, conv, 0.0)
        return carry

    lax.fori_loop(0, 4, input_step, 0)
    arrive(got)
    total = e1s[0]
    for i in range(1, 8):
        total = total + e1s[i]
    e2[...] = total
    f0[z] = e2[rows8(z), :]
    got = exchange(13, z, to_z, lambda p: e2.at[rows8(p), :], f0.at[z])
    lax.fori_loop(4, 8, input_step, 0)
    arrive(got)
    total = f0[0]
    for i in range(1, 8):
        total = total + f0[i]
    f1[...] = total
    fz[rows8(z), :] = total
    arrive(exchange(14, z, to_z, lambda p: f1, fz.at[rows8(z), :]))
    vg[rows64(xc), :] = fz[...]
    arrive(exchange(15, xc, to_xc, lambda p: fz, vg.at[rows64(xc), :]))
    vv_ref[...] = vg[...]
    for copy in sent:
        copy.wait_send()


def body(
    features, conv_weight, qkv_weight, out_weight, cotangent, neighbours, send_slot, recv_slot
):
    wb = jnp.transpose(conv_weight, (0, 2, 1)).reshape(432, 128)
    w2 = jnp.transpose(qkv_weight, (0, 2, 1)).reshape(48, 128)
    vmem = pl.BlockSpec(memory_space=pltpu.VMEM)

    def buf(*shape):
        return pltpu.VMEM(shape, BF)

    def wide(*shape):
        return pltpu.VMEM(shape, F32)

    scratch = [
        buf(SLOTS, CELLS), buf(SLOTS, SLOTS),
        buf(128, EXT), buf(128, 512), buf(2, 16, LAYER), buf(16, CELLS),
        buf(128, 512), buf(8, 16, 512), buf(432, 128), buf(144, EXT),
        buf(16, CELLS), buf(8, 16, 128), buf(8, 16, 128), buf(8, 16, 128), buf(8, 16, 128),
        buf(128, SLOTS), buf(128, SLOTS), buf(64, 128), buf(8, 64, 128),
        buf(SLOTS, 128), buf(8, 128, 256), buf(64, SLOTS), wide(32, SLOTS),
        buf(128, SLOTS), buf(8, 32, 256), buf(8, 32, 128), buf(8, 64, 128),
        buf(8, 32, 128), buf(8, 16, 128), buf(8, 16, 128), buf(8, 16, 128),
        buf(128, SLOTS), buf(128, EXT), buf(16, 512), buf(2, 16, LAYER), buf(128, 512),
        wide(512, 128), buf(8, 16, 128), wide(8, 64, 128), wide(64, 128),
        wide(8, 8, 128), wide(64, 128), wide(8, 128), wide(512, 128),
        pltpu.SemaphoreType.DMA((2, 4, 5)), pltpu.SemaphoreType.DMA((2, 4, 5)),
        pltpu.SemaphoreType.DMA((16, 8)), pltpu.SemaphoreType.DMA((16, 8)),
        pltpu.SemaphoreType.DMA((4,)), pltpu.SemaphoreType.DMA((4,)),
    ]
    block_out, grad_features, sums = pl.pallas_call(
        whole_kernel,
        out_shape=(
            jax.ShapeDtypeStruct((16, SLOTS), BF),
            jax.ShapeDtypeStruct((16, CELLS), F32),
            jax.ShapeDtypeStruct((512, 128), F32),
        ),
        in_specs=[vmem] * 7,
        out_specs=(vmem, vmem, vmem),
        scratch_shapes=scratch,
        compiler_params=pltpu.CompilerParams(
            collective_id=0, has_side_effects=True, vmem_limit_bytes=48 * 1024 * 1024
        ),
    )(
        features, send_slot.reshape(1, CELLS), recv_slot.reshape(1, SLOTS), cotangent,
        wb, w2, out_weight,
    )
    grad_conv = jnp.transpose(sums[0:432].reshape(27, 16, 128), (0, 2, 1))
    grad_qkv = jnp.transpose(sums[432:480].reshape(3, 16, 128), (0, 2, 1))
    return (block_out, grad_features, grad_conv, grad_qkv, sums[480:496])


def solution(mesh):
    torus = Mesh(mesh.devices.reshape(8, 4, 2, mesh.shape["ch"]), ("vox_0", "vox_1", "vox_2", "ch"))
    placed = (
        P("ch", VOX),
        P(None, None, "ch"),
        P(None, None, "ch"),
        P("ch", None),
        P("ch", VOX),
        P(None, VOX),
        P(VOX),
        P(VOX),
    )
    return jax.shard_map(
        body,
        mesh=torus,
        in_specs=placed,
        out_specs=(
            P("ch", VOX),
            P("ch", VOX),
            P(None, None, "ch"),
            P(None, None, "ch"),
            P("ch", None),
        ),
        check_vma=False,
    )
```

time: 364 us -> 128 us (0.35)
  Pallas kernels: 0 us -> 118 us
  blocking collectives: 109 us -> 0 us
  starting transfers between devices: 90.4 us -> 0 us
  local copies, waits for them, and re-layouts: 55.2 us -> 8.57 us
  matrix products: 38.2 us -> 0 us
  waiting for transfers between devices: 28.1 us -> 0 us
  other arithmetic: 25 us -> 0 us
  between operations: 15.1 us -> 0.66 us
    pallas_call x0 -> x1, Pallas kernels: none -> 118 us  [body(): pl.pallas_call(whole_kernel, out_shape=(jax.ShapeDtypeStruct((16, SLOTS),...]
    all_gather x4 -> x0, blocking collectives: 99 us -> none  [the longest x2 58.1 us: channels(): return lax.all_gather(field, 'ch', axis=0, tiled=True)]
    all_to_all x5 -> x0, starting transfers between devices: 68.4 us -> none  [the longest x2 39.6 us: regroup(): lax.all_to_all(slots_buffer, VOX, split_axis=1, concat_axis=1, tiled=True)]
    dot_general x73 -> x0, matrix products: 38.2 us -> none  [the longest x27 13.9 us: body(): jnp.dot(own_weight[which], columns, preferred_element_type=jnp.float32)]
    ppermute x4 -> x0, starting transfers between devices: 21.9 us -> none  [the longest x2 17.9 us: extended(): before = lax.ppermute(last, axis, up)]
    gather x4 -> x0, local copies, waits for them, and re-layouts: 19.7 us -> none  [regroup(): picked = jnp.take(arrived, jnp.maximum(in_slot, 0), axis=1)]
    unnamed x26 -> x0, other arithmetic: 19.5 us -> none
    all_to_all x5 -> x0, waiting for transfers between devices: 16.9 us -> none  [the longest x2 8.53 us: regroup(): lax.all_to_all(slots_buffer, VOX, split_axis=1, concat_axis=1, tiled=True)]
  transfers between devices with their start and end apart: 11 -> 0, of which waited for: 4 -> 0; matrix products, arithmetic and copies ran while one was open for 13% -> 0% of each run, Pallas kernels for 0% -> 0%
where the time goes in v1:
time: 128 us; the launch traced here: 127 us
  Pallas kernels  118 us (92%)
  local copies, waits for them, and re-layouts  8.57 us (7%)
    pallas_call x1, Pallas kernels, body(): pl.pallas_call(whole_kernel, out_shape=(jax.ShapeDtypeStruct((16, SLOTS),...  118 us
    unnamed x16, local copies, waits for them, and re-layouts  6.66 us

profile of v1, /device:TPU:1, one launch (start us, length us, event | category | flops | bytes accessed | tf_op | source)
XLA Modules:
  0.0 127.3 jit_solution(15208174187211113218)
XLA Ops:
  0.6 0.0 copy-start.5
  0.6 0.7 copy-done.5
  1.3 0.0 copy-start
  1.3 0.9 copy-done
  2.2 0.0 copy-start.1
  2.2 0.9 copy-done.1
  3.1 0.0 copy-start.2
  3.1 0.8 copy-done.2
  3.9 0.0 copy-start.3
  3.9 0.7 copy-done.3
  4.6 0.0 copy-start.4
  4.6 0.7 copy-done.4
  5.3 0.0 copy-start.6
  5.3 0.7 copy-done.6
  6.0 118.0 %shard_map.110 = (bf16[16,1024]{1,0:T(8,128)(2,1)S(1)}, f32[16,4096]{1,0:T(8,128)S(1)}, f32[512,128]{1,0:T(8,128)S(1)}) custom-call(bf16[16,4096]{1,0:T(8,128)(2,1)S(1)} %copy-done, s32[1,4096]{1,0:T(1,128)S(1)} %bitcast.15, s32[1,1024]{1,0:T(1,128)S(1)} %bitcast.17, bf16[16,1024]{1,0:T(8,128)(2,1)S(1)} %copy-done.2, bf16[432,128]{1,0:T(8,128)(2,1)S(1)} %bitcast.14, ...), custom_call_target="tpu_custom_call" | custom-call | tf_op jit(solution)/shard_map/pallas_call | solution.py:501
  124.0 0.6 slice.11
  124.6 0.6 slice.10
  125.2 0.7 slice.9
  125.9 0.6 copy.14
  126.6 0.7 copy.15
Async XLA Ops:
  0.6 0.7 copy-start.5
  1.3 0.9 copy-start
  2.2 0.9 copy-start.1
  3.1 0.8 copy-start.2
  3.9 0.7 copy-start.3
  4.6 0.7 copy-start.4
  5.3 0.7 copy-start.6

commit v2 on v1

v2 whole, which is shorter than its diff:
```python
import jax
import jax.numpy as jnp
from jax import lax
from jax.experimental import pallas as pl
from jax.experimental.pallas import tpu as pltpu
from jax.sharding import Mesh
from jax.sharding import PartitionSpec as P

MESH = pl.DeviceIdType.MESH
VOX = ("vox_0", "vox_1", "vox_2")
BF = jnp.bfloat16
F32 = jnp.float32
CELLS = 4096
LAYER = 256
EXT = CELLS + 2 * LAYER
SLOTS = 1024
ORDER = (4, 3, 5, 2, 6, 1, 7)


def nn(a, b):
    return jnp.dot(a, b, preferred_element_type=F32)


def nt(a, b):
    return lax.dot_general(a, b, (((1,), (1,)), ((), ())), preferred_element_type=F32)


def tn(a, b):
    return lax.dot_general(a, b, (((0,), (0,)), ((), ())), preferred_element_type=F32)


def lanes(shape):
    return lax.broadcasted_iota(jnp.int32, shape, 1)


def swap_blocks(tiles):
    flat = tiles.reshape(128, 128)
    turned = [flat if s == 0 else pltpu.roll(flat, s * 16, 1) for s in range(8)]
    block = lanes((16, 128)) // 16
    out = []
    for j in range(8):
        tile = turned[(0 - j) % 8][0:16]
        for i in range(1, 8):
            tile = jnp.where(block == i, turned[(i - j) % 8][i * 16 : i * 16 + 16], tile)
        out.append(tile)
    return out


def in_layer(width, dy, dz):
    cell = lanes((16, width))
    row = (cell // 16) % 16 + dy
    col = cell % 16 + dz
    return (row >= 0) & (row < 16) & (col >= 0) & (col < 16)


def whole_kernel(
    f_in, ss_in, rs_in, cot_in, wb_in, w2_in, ow_in,
    bo_out, gf_out, vv_out,
    bo_ref, gf_ref, vv_ref, f_ref, ss_ref, rs_ref, cot_ref, wb_ref, w2_ref, ow_ref,
    onehot, pick, fx, hx, hl, fm, fc, wt, aw, w9, s27, s9c, layer, s1acc,
    s1, a1, t1, a2, gw, cw, mine2, ww,
    kvt, qq, gg, qkv, gaw, lg, pr, sc, pk, acc, big, xs, ys, u1, c2, v1, d1,
    glw, gx, hf, hl2, hg, vs, e0, half, pair, quad, own64, zsrc, zall, back64, back256,
    in_sem, out_sem, ex_s, ex_r, halo_s, halo_r, red_s, red_r,
):
    z = lax.axis_index("vox_0")
    x = lax.axis_index("vox_1")
    core = lax.axis_index("vox_2")
    xc = x * 2 + core
    y = lax.axis_index("ch")
    d = z * 8 + xc

    def to_y(p):
        return {"ch": p}

    def to_z(p):
        return {"vox_0": p}

    def to_x(p):
        return {"vox_1": p}

    def to_xc(p):
        return {"vox_1": p // 2, "vox_2": lax.rem(p, 2)}

    def to_d(p):
        return {"vox_0": p // 8, "vox_1": lax.rem(p, 8) // 2, "vox_2": lax.rem(p, 2)}

    after, before = lax.rem(d + 1, 64), lax.rem(d + 63, 64)

    barrier = pltpu.get_barrier_semaphore()
    for r in range(1, 8):
        for me, where in ((y, to_y), (z, to_z), (xc, to_xc)):
            pl.semaphore_signal(
                barrier, inc=1, device_id=where(lax.rem(me + r, 8)), device_id_type=MESH
            )
    for p in (after, before):
        pl.semaphore_signal(barrier, inc=1, device_id=to_d(p), device_id_type=MESH)

    loads = [
        pltpu.make_async_copy(src, dst, in_sem.at[i])
        for i, (src, dst) in enumerate(
            (
                (ss_in, ss_ref), (f_in, f_ref), (wb_in, wb_ref), (rs_in, rs_ref),
                (cot_in, cot_ref), (w2_in, w2_ref), (ow_in, ow_ref),
            )
        )
    ]
    for load in loads:
        load.start()

    fresh, old = [], []

    def send(src, dst, s_sem, r_sem, where):
        copy = pltpu.make_async_remote_copy(
            src_ref=src, dst_ref=dst, send_sem=s_sem, recv_sem=r_sem,
            device_id=where, device_id_type=MESH,
        )
        copy.start()
        fresh.append(copy)
        return copy

    def drain():
        for copy in old:
            copy.wait_send()
        old[:] = fresh
        fresh.clear()

    def exchange(phase, me, where, src_of, dst):
        copies = []
        for r in ORDER:
            p = lax.rem(me + r, 8)
            copies.append(
                send(src_of(p), dst, ex_s.at[phase, r], ex_r.at[phase, r], where(p))
            )
        return copies

    def arrive(copies):
        for copy in copies:
            copy.wait_recv()

    def rows16(b):
        return pl.ds(pl.multiple_of(b * 16, 16), 16)

    def tile(b):
        return pl.ds(pl.multiple_of(b * 128, 128), 128)

    def span(i, start=0, size=512):
        return pl.ds(pl.multiple_of(i * 512 + start, 256), size)

    mine = rows16(y)
    loads[0].wait()

    def onehot_step(i, carry):
        at = pl.multiple_of(i * 16, 16)
        ids = lax.broadcasted_iota(jnp.int32, (16, CELLS), 0) + at
        onehot[pl.ds(at, 16), :] = jnp.where(ids == ss_ref[...], 1.0, 0.0).astype(BF)
        return carry

    lax.fori_loop(0, 64, onehot_step, 0)

    loads[1].wait()
    fm[...] = jnp.where(ss_ref[...] >= 0, f_ref[...].astype(F32), 0.0).astype(BF)

    def compact_step(i, carry):
        at = pl.multiple_of(i * 256, 256)
        fc[mine, pl.ds(at, 256)] = nt(fm[...], onehot[pl.ds(at, 256), :]).astype(BF)
        return carry

    lax.fori_loop(0, 4, compact_step, 0)

    loads[2].wait()
    weights = jnp.concatenate([wb_ref[...].astype(F32), jnp.zeros((80, 128), F32)], axis=0)
    for t in range(4):
        wt[:, t * 128 : t * 128 + 128] = weights[t * 128 : t * 128 + 128, :].T.astype(BF)

    pl.semaphore_wait(barrier, 23)
    got = exchange(0, y, to_y, lambda p: fc.at[mine, :], fc.at[mine, :])
    halo = [
        send(fm.at[:, CELLS - LAYER : CELLS], hl.at[0], halo_s.at[0], halo_r.at[0], to_d(after)),
        send(fm.at[:, 0:LAYER], hl.at[1], halo_s.at[1], halo_r.at[1], to_d(before)),
    ]
    got_aw = exchange(11, y, to_y, lambda p: wt.at[rows16(p), :], aw.at[y])

    aw[y] = wt[mine, :]
    for load in loads[3:]:
        load.wait()
    live = rs_ref[...] >= 0
    cw[mine, :] = jnp.where(live, cot_ref[...].astype(F32), 0.0).astype(BF)
    mine2[0:48, :] = w2_ref[...]
    mine2[48:64, :] = ow_ref[...]
    ww[y] = mine2[...]
    source = rs_ref[...]
    route = (source >> 4) & 7
    spot = jnp.where(live, route * 128 + ((source >> 7) & 7) * 16 + (source & 15), -1)

    arrive(halo)
    hx[mine, 0:LAYER] = jnp.where(d == 0, 0.0, hl[0].astype(F32)).astype(BF)
    hx[mine, LAYER : 2 * LAYER] = jnp.where(d == 63, 0.0, hl[1].astype(F32)).astype(BF)
    got_hx = exchange(12, y, to_y, lambda p: hx.at[mine, :], hx.at[mine, :])

    taps = [(dy, dz) for dy in (-1, 0, 1) for dz in (-1, 0, 1)]

    def shifted(values, width, put):
        for j, (dy, dz) in enumerate(taps):
            shift = -(dy * 16 + dz) % width
            slab = pltpu.roll(values, shift, 1) if shift else values
            slab = jnp.where(in_layer(width, dy, dz), slab, 0.0).astype(BF)
            for dx in range(3):
                put(dx, dx * 144 + j * 16, slab)

    def shifted_step(i, carry):
        def put(dx, row, slab):
            s27[row : row + 16, span(i, (3 - dx) * LAYER)] = slab

        shifted(fm[:, span(i)].astype(F32), 512, put)
        return carry

    lax.fori_loop(0, 8, shifted_step, 0)
    edges = hx[mine, :].astype(F32)

    def put_left(dx, row, slab):
        s27[row : row + 16, (2 - dx) * LAYER : (3 - dx) * LAYER] = slab[:, 0:LAYER]

    def put_right(dx, row, slab):
        s27[row : row + 16, (19 - dx) * LAYER : (20 - dx) * LAYER] = slab[:, LAYER : 2 * LAYER]

    shifted(edges, 512, put_left)
    shifted(edges, 512, put_right)

    def s9c_step(i, carry):
        at = pl.multiple_of(i * 256, 256)
        s9c[:, pl.ds(at, 256)] = nt(
            s27[:, 512 : 512 + CELLS], onehot[pl.ds(at, 256), :]
        ).astype(BF)
        return carry

    lax.fori_loop(0, 4, s9c_step, 0)

    def pick_step(i, carry):
        at = pl.multiple_of(i * 16, 16)
        ids = lax.broadcasted_iota(jnp.int32, (16, SLOTS), 0) + at
        pick[pl.ds(at, 16), :] = jnp.where(ids == spot, 1.0, 0.0).astype(BF)
        return carry

    lax.fori_loop(0, 64, pick_step, 0)
    qq[...] = jnp.zeros((128, SLOTS), BF)
    gg[...] = jnp.zeros((128, SLOTS), BF)
    s1acc[...] = jnp.zeros((16, SLOTS), F32)
    acc[...] = jnp.zeros((32, SLOTS), F32)

    arrive(got_aw)
    for t in range(4):
        for k, part in enumerate(swap_blocks(aw[:, :, t * 128 : t * 128 + 128].astype(F32))):
            if t * 8 + k < 27:
                at = (t * 8 + k) * 16
                w9[at : at + 16, :] = part.astype(BF)

    arrive(got)
    got_ww = exchange(1, y, to_y, lambda p: mine2, ww.at[y])
    got_cw = exchange(2, y, to_y, lambda p: cw.at[mine, :], cw.at[mine, :])
    drain()

    def expand(src, dst, i):
        dst[:, span(i, LAYER)] = nn(src[...], onehot[:, span(i)]).astype(BF)

    def conv(i):
        total = None
        for dx in range(3):
            field = fx[:, span(i, dx * LAYER)]
            term = nn(w9[dx * 144 : dx * 144 + 144, :], field)
            total = term if total is None else total + term
        out = fm[:, span(i)].astype(F32)
        summed = jnp.zeros((16, 512), F32)
        for j, (dy, dz) in enumerate(taps):
            shift = -(dy * 16 + dz) % 512
            slab = total[j * 16 : j * 16 + 16]
            slab = pltpu.roll(slab, shift, 1) if shift else slab
            summed = summed + jnp.where(in_layer(512, dy, dz), slab, 0.0)
        layer[:, span(i)] = (out + summed).astype(BF)

    def pack(i):
        s1acc[...] += nt(layer[:, span(i)], onehot[:, span(i)])

    for i in range(3):
        expand(fc, fx, i)
    arrive(got_hx)
    fx[:, 0:LAYER] = hx[:, 0:LAYER]
    fx[:, LAYER + CELLS : EXT] = hx[:, LAYER : 2 * LAYER]
    conv(0)

    def conv_step(i, carry):
        pack(i - 1)
        conv(i)
        expand(fc, fx, i + 2)
        return carry

    lax.fori_loop(1, 6, conv_step, 0)
    pack(5)
    conv(6)
    pack(6)
    conv(7)
    pack(7)
    packed = s1acc[...].astype(BF)
    for t in range(8):
        s1[t] = packed[:, t * 128 : t * 128 + 128]
    a1[z] = s1[z]
    got = exchange(3, z, to_z, lambda p: s1.at[p], a1.at[z])

    drain()
    arrive(got)
    for j, part in enumerate(swap_blocks(a1[...].astype(F32))):
        t1[j] = part.astype(BF)
    a2[xc] = t1[xc]
    got = exchange(4, xc, to_xc, lambda p: t1.at[p], a2.at[xc])
    drain()
    arrive(got)
    arrived = jnp.concatenate([a2[i] for i in range(8)], axis=1)
    gw[mine, :] = nn(arrived, pick[...]).astype(BF)
    got = exchange(5, y, to_y, lambda p: gw.at[mine, :], gw.at[mine, :])
    drain()
    arrive(got_cw)
    arrive(got_ww)
    ga = nn(ow_ref[...], cw[...]).astype(BF)
    gaw[...] = ga
    gg[32:48, :] = (ga.astype(F32) * 0.25).astype(BF)
    arrive(got)

    whole = gw[...].astype(F32)
    mean = jnp.mean(whole, axis=0, keepdims=True)
    centred = whole - mean
    var = jnp.mean(centred * centred, axis=0, keepdims=True)
    normed = (centred * lax.rsqrt(var + 1e-05)).astype(BF)
    big[...] = normed
    rows = nn(w2_ref[...], normed).astype(BF)
    qkv[...] = rows
    qq[0:16, :] = (rows[0:16].astype(F32) * 0.25).astype(BF)
    row = lax.broadcasted_iota(jnp.int32, (16, SLOTS), 0)
    qq[16:32, :] = jnp.where(row == 0, 1.0, 0.0).astype(BF)
    bias = jnp.where((row == 0) & (~live), -1e30, 0.0)
    stacked = jnp.concatenate(
        [
            rows[16:32].astype(F32),
            bias,
            rows[32:48].astype(F32),
            jnp.zeros((80, SLOTS), F32),
        ],
        axis=0,
    )
    for t in range(8):
        kvt[t * 128 : t * 128 + 128, :] = stacked[:, t * 128 : t * 128 + 128].T.astype(BF)

    def attend_step(i, carry):
        at = pl.ds(pl.multiple_of(i * 256, 256), 256)
        top = None
        for c in range(4):
            cells = slice(c * 256, c * 256 + 256)
            logits = nn(kvt[cells, :], qq[:, at])
            lg[cells, :] = logits
            most = jnp.max(logits.reshape(32, 8, 256), axis=0)
            top = most if top is None else jnp.maximum(top, most)
        top = jnp.max(top, axis=0, keepdims=True)
        total = jnp.zeros((8, 256), F32)
        for c in range(16):
            cells = slice(c * 64, c * 64 + 64)
            exponents = jnp.exp(lg[cells, :] - top)
            lg[cells, :] = exponents
            total = total + jnp.sum(exponents.reshape(8, 8, 256), axis=0)
        inverse_total = 1.0 / jnp.sum(total, axis=0, keepdims=True)
        for c in range(16):
            cells = slice(c * 64, c * 64 + 64)
            pr[cells, :] = (lg[cells, :] * inverse_total).astype(BF)
        attended = nn(qkv[32:48, :], pr[...])
        pk[0:16, at] = attended.astype(BF)
        inner = jnp.sum(attended * gg[32:48, at].astype(F32), axis=0, keepdims=True)
        acc[16:32, :] += nt(gaw[:, at], pr[...])
        for c in range(4):
            cells = slice(c * 256, c * 256 + 256)
            grad_logits = nn(kvt[cells, :], gg[:, at])
            sc[cells, :] = (pr[cells, :].astype(F32) * (grad_logits - inner)).astype(BF)
        pk[16:32, at] = nn(qkv[16:32, :], sc[...]).astype(BF)
        acc[0:16, :] += nt(qkv[0:16, at], sc[...])
        return carry

    lax.fori_loop(0, 4, attend_step, 0)
    pk[32:64, :] = acc[...].astype(BF)

    ys[y] = pk[:, tile(y)]
    got = exchange(6, y, to_y, lambda p: pk.at[:, tile(p)], ys.at[y])
    drain()
    vs[432:480, :] = nt(pk[16:64, :], big[...])
    vs[480:496, :] = nt(pk[0:16, :], cw[...])
    vs[496:512, :] = jnp.zeros((16, 128), F32)
    own_slots = tile(y)
    part = gw[:, own_slots].astype(F32)
    mean = jnp.mean(part, axis=0, keepdims=True)
    centred = part - mean
    var = jnp.mean(centred * centred, axis=0, keepdims=True)
    inverse = lax.rsqrt(var + 1e-05)
    normal = centred * inverse
    cot = cw[:, own_slots].astype(F32)
    live_part = rs_ref[:, own_slots] >= 0
    arrive(got)
    mixed = tn(ww[:, 48:64, :].reshape(128, 128), ys[:, 0:16, :].reshape(128, 128))
    grad = None
    for i in range(3):
        term = tn(
            ww[:, i * 16 : i * 16 + 16, :].reshape(128, 128),
            ys[:, 16 + i * 16 : 32 + i * 16, :].reshape(128, 128),
        )
        grad = term if grad is None else grad + term
    grad = grad.astype(BF).astype(F32)
    grad_ln = inverse * (
        grad
        - jnp.mean(grad, axis=0, keepdims=True)
        - normal * jnp.mean(grad * normal, axis=0, keepdims=True)
    )
    back = jnp.where(live_part, cot + grad_ln, 0.0).astype(BF)
    block = jnp.where(live_part, part + mixed, 0.0).astype(BF)
    xs[:, 0:16, :] = back.reshape(8, 16, 128)
    xs[:, 16:32, :] = block.reshape(8, 16, 128)
    u1[y] = xs[y]
    got = exchange(7, y, to_y, lambda p: xs.at[p], u1.at[y])
    drain()
    arrive(got)
    grad_grouped = jnp.concatenate([u1[i, 0:16] for i in range(8)], axis=1)
    spread = nt(grad_grouped, pick[...])
    for t in range(8):
        c2[t] = spread[:, t * 128 : t * 128 + 128].astype(BF)
    v1[xc] = c2[xc]
    got = exchange(8, xc, to_xc, lambda p: c2.at[p], v1.at[xc])
    drain()
    bo_ref[...] = jnp.concatenate([u1[i, 16:32] for i in range(8)], axis=1)
    stores = [
        pltpu.make_async_copy(src, dst, out_sem.at[i])
        for i, (src, dst) in enumerate(((bo_ref, bo_out), (gf_ref, gf_out), (vv_ref, vv_out)))
    ]
    stores[0].start()
    arrive(got)
    for j, piece in enumerate(swap_blocks(v1[...].astype(F32))):
        d1[j] = piece.astype(BF)
    e0[z] = d1[z]
    got = exchange(9, z, to_z, lambda p: d1.at[p], e0.at[z])
    drain()
    arrive(got)
    slots = jnp.concatenate([e0[i] for i in range(8)], axis=1)
    glw[mine, :] = slots
    got = exchange(10, y, to_y, lambda p: glw.at[mine, :], glw.at[mine, :])
    drain()
    hf[:, 0:LAYER] = nn(slots, onehot[:, 0:LAYER]).astype(BF)
    hf[:, LAYER : 2 * LAYER] = nn(slots, onehot[:, CELLS - LAYER : CELLS]).astype(BF)
    halo = [
        send(hf.at[:, LAYER : 2 * LAYER], hl2.at[0], halo_s.at[2], halo_r.at[2], to_d(after)),
        send(hf.at[:, 0:LAYER], hl2.at[1], halo_s.at[3], halo_r.at[3], to_d(before)),
    ]
    arrive(halo)
    hg[mine, 0:LAYER] = jnp.where(d == 0, 0.0, hl2[0].astype(F32)).astype(BF)
    hg[mine, LAYER : 2 * LAYER] = jnp.where(d == 63, 0.0, hl2[1].astype(F32)).astype(BF)
    got_halo = exchange(13, y, to_y, lambda p: hg.at[mine, :], hg.at[mine, :])
    arrive(got)

    vs[0:432, :] = nt(s9c[...], glw[...])

    def rows64(b):
        return pl.ds(pl.multiple_of(b * 64, 64), 64)

    def rows256(b):
        return pl.ds(pl.multiple_of(b * 256, 256), 256)

    def grad_expand(i, carry):
        expand(glw, gx, i)
        return carry

    def input_step(i, carry):
        total = None
        for dx in range(3):
            field = gx[:, span(i, (2 - dx) * LAYER)]
            term = nn(wb_ref[dx * 144 : dx * 144 + 144, :], field)
            total = term if total is None else total + term
        conv = jnp.zeros((16, 512), F32)
        for j, (dy, dz) in enumerate(taps):
            shift = (dy * 16 + dz) % 512
            slab = total[j * 16 : j * 16 + 16]
            slab = pltpu.roll(slab, shift, 1) if shift else slab
            conv = conv + jnp.where(in_layer(512, -dy, -dz), slab, 0.0)
        own_grad = gx[mine, span(i, LAYER)].astype(F32)
        gf_ref[:, span(i)] = own_grad + jnp.where(ss_ref[:, span(i)] >= 0, conv, 0.0)
        return carry

    def pair_send(src, dst, n):
        return send(src, dst, red_s.at[n], red_r.at[n], {"vox_2": 1 - core})

    def x_send(src_of, dst, n):
        copies = []
        for r in (2, 1, 3):
            p = lax.rem(x + r, 4)
            copies.append(send(src_of(p), dst, red_s.at[n + r], red_r.at[n + r], to_x(p)))
        return copies

    got = [pair_send(vs.at[rows256(1 - core), :], half, 0)]
    arrive(got)
    pair[...] = vs[rows256(core), :] + half[...]
    quad[x] = pair[rows64(x), :]
    got = x_send(lambda p: pair.at[rows64(p), :], quad.at[x], 0)
    drain()
    lax.fori_loop(0, 8, grad_expand, 0)
    arrive(got)
    own64[...] = (quad[0] + quad[1] + quad[2] + quad[3]).astype(BF)
    zsrc[z] = own64[...]
    got = exchange(14, z, to_z, lambda p: own64, zsrc.at[z])
    drain()
    arrive(got_halo)
    gx[:, 0:LAYER] = hg[:, 0:LAYER]
    gx[:, LAYER + CELLS : EXT] = hg[:, LAYER : 2 * LAYER]
    lax.fori_loop(0, 6, input_step, 0)
    arrive(got)
    total = zsrc[0].astype(F32)
    for i in range(1, 8):
        total = total + zsrc[i].astype(F32)
    zall[...] = total
    back256[rows64(x), :] = total
    got = x_send(lambda p: zall, back256.at[rows64(x), :], 4)
    lax.fori_loop(6, 8, input_step, 0)
    stores[1].start()
    arrive(got)
    got = [pair_send(back256, back64, 8)]
    vv_ref[rows256(core), :] = back256[...]
    drain()
    arrive(got)
    vv_ref[rows256(1 - core), :] = back64[...]
    stores[2].start()
    drain()
    drain()
    for store in stores:
        store.wait()


def store_kernel(
    bo_ref, gf_ref, vv_ref, bo_out, gf_out, gc_out, gq_out, go_out, bo, gf, vv, in_sem, out_sem
):
    loads = [
        pltpu.make_async_copy(src, dst, in_sem.at[i])
        for i, (src, dst) in enumerate(((gf_ref, gf), (vv_ref, vv), (bo_ref, bo)))
    ]
    stores = [
        pltpu.make_async_copy(src, dst, out_sem.at[i])
        for i, (src, dst) in enumerate(
            (
                (gf, gf_out), (vv.at[0:432, :], gc_out), (vv.at[432:480, :], gq_out),
                (vv.at[480:496, :], go_out), (bo, bo_out),
            )
        )
    ]
    for load in loads:
        load.start()
    for load, behind in zip(loads, (stores[0:1], stores[1:4], stores[4:5])):
        load.wait()
        for store in behind:
            store.start()
    for store in stores:
        store.wait()


def body(
    features, conv_weight, qkv_weight, out_weight, cotangent, neighbours, send_slot, recv_slot
):
    wb = jnp.transpose(conv_weight, (0, 2, 1)).reshape(432, 128)
    w2 = jnp.transpose(qkv_weight, (0, 2, 1)).reshape(48, 128)

    def buf(*shape):
        return pltpu.VMEM(shape, BF)

    def wide(*shape):
        return pltpu.VMEM(shape, F32)

    scratch = [
        buf(16, SLOTS), wide(16, CELLS), wide(512, 128),
        buf(16, CELLS), pltpu.VMEM((1, CELLS), jnp.int32), pltpu.VMEM((1, SLOTS), jnp.int32),
        buf(16, SLOTS), buf(432, 128), buf(48, 128), buf(16, 128),
        buf(SLOTS, CELLS), buf(SLOTS, SLOTS),
        buf(128, EXT), buf(128, 512), buf(2, 16, LAYER), buf(16, CELLS),
        buf(128, SLOTS), buf(128, 512), buf(8, 16, 512), buf(432, 128),
        buf(432, 20 * LAYER), buf(432, SLOTS), buf(16, CELLS), wide(16, SLOTS),
        buf(8, 16, 128), buf(8, 16, 128), buf(8, 16, 128), buf(8, 16, 128),
        buf(128, SLOTS), buf(128, SLOTS), buf(64, 128), buf(8, 64, 128),
        buf(SLOTS, 128), buf(128, SLOTS), buf(128, SLOTS), buf(48, SLOTS),
        buf(16, SLOTS), wide(SLOTS, 256), buf(SLOTS, 256), buf(SLOTS, 256),
        buf(64, SLOTS), wide(32, SLOTS), buf(128, SLOTS),
        buf(8, 32, 128), buf(8, 64, 128), buf(8, 32, 128),
        buf(8, 16, 128), buf(8, 16, 128), buf(8, 16, 128),
        buf(128, SLOTS), buf(128, EXT), buf(16, 512), buf(2, 16, LAYER), buf(128, 512),
        wide(512, 128), buf(8, 16, 128), wide(256, 128), wide(256, 128),
        wide(4, 64, 128), buf(64, 128), buf(8, 64, 128), wide(64, 128),
        wide(256, 128), wide(256, 128),
        pltpu.SemaphoreType.DMA((7,)), pltpu.SemaphoreType.DMA((3,)),
        pltpu.SemaphoreType.DMA((15, 8)), pltpu.SemaphoreType.DMA((15, 8)),
        pltpu.SemaphoreType.DMA((4,)), pltpu.SemaphoreType.DMA((4,)),
        pltpu.SemaphoreType.DMA((9,)), pltpu.SemaphoreType.DMA((9,)),
    ]
    hbm = pl.BlockSpec(memory_space=pltpu.HBM)
    block_out, grad_features, sums = pl.pallas_call(
        whole_kernel,
        out_shape=(
            jax.ShapeDtypeStruct((16, SLOTS), BF),
            jax.ShapeDtypeStruct((16, CELLS), F32),
            jax.ShapeDtypeStruct((512, 128), F32),
        ),
        in_specs=[hbm] * 7,
        out_specs=(hbm, hbm, hbm),
        scratch_shapes=scratch,
        compiler_params=pltpu.CompilerParams(
            collective_id=0, has_side_effects=True, vmem_limit_bytes=67043328
        ),
    )(
        features, send_slot.reshape(1, CELLS), recv_slot.reshape(1, SLOTS), cotangent,
        wb, w2, out_weight,
    )
    block_out, grad_features, grad_conv, grad_qkv, grad_out = pl.pallas_call(
        store_kernel,
        out_shape=(
            jax.ShapeDtypeStruct((16, SLOTS), BF),
            jax.ShapeDtypeStruct((16, CELLS), F32),
            jax.ShapeDtypeStruct((432, 128), F32),
            jax.ShapeDtypeStruct((48, 128), F32),
            jax.ShapeDtypeStruct((16, 128), F32),
        ),
        in_specs=[hbm] * 3,
        out_specs=(hbm,) * 5,
        scratch_shapes=[
            buf(16, SLOTS), wide(16, CELLS), wide(512, 128),
            pltpu.SemaphoreType.DMA((3,)), pltpu.SemaphoreType.DMA((5,)),
        ],
        compiler_params=pltpu.CompilerParams(vmem_limit_bytes=67043328),
    )(block_out, grad_features, sums)
    grad_conv = jnp.transpose(grad_conv.reshape(27, 16, 128), (0, 2, 1))
    grad_qkv = jnp.transpose(grad_qkv.reshape(3, 16, 128), (0, 2, 1))
    return (block_out, grad_features, grad_conv, grad_qkv, grad_out)


def solution(mesh):
    torus = Mesh(mesh.devices.reshape(8, 4, 2, mesh.shape["ch"]), ("vox_0", "vox_1", "vox_2", "ch"))
    placed = (
        P("ch", VOX),
        P(None, None, "ch"),
        P(None, None, "ch"),
        P("ch", None),
        P("ch", VOX),
        P(None, VOX),
        P(VOX),
        P(VOX),
    )
    return jax.shard_map(
        body,
        mesh=torus,
        in_specs=placed,
        out_specs=(
            P("ch", VOX),
            P("ch", VOX),
            P(None, None, "ch"),
            P(None, None, "ch"),
            P("ch", None),
        ),
        check_vma=False,
    )
```

time: 128 us -> 108 us (0.84)
  Pallas kernels: 118 us -> 107 us
  local copies, waits for them, and re-layouts: 8.57 us -> 0 us
    pallas_call x1, Pallas kernels: 118 us -> 105 us  [body(): pl.pallas_call(whole_kernel, out_shape=(jax.ShapeDtypeStruct((16, SLOTS),...]
    unnamed x16 -> x0, local copies, waits for them, and re-layouts: 6.66 us -> none
    slice x3 -> x0, local copies, waits for them, and re-layouts: 1.91 us -> none  [the longest x1 0.7 us: body(): grad_conv = jnp.transpose(sums[0:432].reshape(27, 16, 128), (0, 2, 1))]
    pallas_call x0 -> x1, Pallas kernels: none -> 1.81 us  [body(): pl.pallas_call(store_kernel, out_shape=(jax.ShapeDtypeStruct((16, SLOTS),...]
where the time goes in v2:
time: 108 us; the launch traced here: 107 us
  Pallas kernels  107 us (99%)
    pallas_call x1, Pallas kernels, body(): pl.pallas_call(whole_kernel, out_shape=(jax.ShapeDtypeStruct((16, SLOTS),...  105 us

profile of v2, /device:TPU:1, one launch (start us, length us, event | category | flops | bytes accessed | tf_op | source)
XLA Modules:
  0.0 107.4 jit_solution(17317732761925051013)
XLA Ops:
  0.6 105.0 %shard_map.110 = (bf16[16,1024]{1,0:T(8,128)(2,1)}, f32[16,4096]{1,0:T(8,128)}, f32[512,128]{1,0:T(8,128)}) custom-call(bf16[16,4096]{1,0:T(8,128)(2,1)} %f_in.1, s32[1,4096]{1,0:T(1,128)} %bitcast.15, s32[1,1024]{1,0:T(1,128)} %bitcast.17, bf16[16,1024]{1,0:T(8,128)(2,1)} %cot_in.1, bf16[432,128]{1,0:T(8,128)(2,1)} %bitcast.14, bf16[48,128]{1,0:T(8,128)(2,1)} %bitcast.16, ...), custom_call_target="tpu_custom_call" | custom-call | tf_op jit(solution)/shard_map/pallas_call | solution.py:600
  105.6 1.8 %shard_map.111 = (bf16[16,1024]{1,0:T(8,128)(2,1)}, f32[16,4096]{1,0:T(8,128)}, f32[432,128]{1,0:T(8,128)}, f32[48,128]{1,0:T(8,128)}, f32[16,128]{1,0:T(8,128)}) custom-call(bf16[16,1024]{1,0:T(8,128)(2,1)} %get-tuple-element.13.bo_ref, f32[16,4096]{1,0:T(8,128)} %get-tuple-element.14.gf_ref, f32[512,128]{1,0:T(8,128)} %get-tuple-element.15.vv_ref), custom_call_target="tpu_custom_call" | custom-call | tf_op jit(solution)/shard_map/pallas_call | solution.py:617

commit v3 on v2

--- a/solution.py
+++ b/solution.py
@@ -161,25 +161,25 @@
     loads[1].wait()
     fm[...] = jnp.where(ss_ref[...] >= 0, f_ref[...].astype(F32), 0.0).astype(BF)
 
-    def compact_step(i, carry):
-        at = pl.multiple_of(i * 256, 256)
-        fc[mine, pl.ds(at, 256)] = nt(fm[...], onehot[pl.ds(at, 256), :]).astype(BF)
-        return carry
-
-    lax.fori_loop(0, 4, compact_step, 0)
-
     loads[2].wait()
     weights = jnp.concatenate([wb_ref[...].astype(F32), jnp.zeros((80, 128), F32)], axis=0)
     for t in range(4):
         wt[:, t * 128 : t * 128 + 128] = weights[t * 128 : t * 128 + 128, :].T.astype(BF)
 
     pl.semaphore_wait(barrier, 23)
-    got = exchange(0, y, to_y, lambda p: fc.at[mine, :], fc.at[mine, :])
     halo = [
         send(fm.at[:, CELLS - LAYER : CELLS], hl.at[0], halo_s.at[0], halo_r.at[0], to_d(after)),
         send(fm.at[:, 0:LAYER], hl.at[1], halo_s.at[1], halo_r.at[1], to_d(before)),
     ]
     got_aw = exchange(11, y, to_y, lambda p: wt.at[rows16(p), :], aw.at[y])
+    def compact_step(i, carry):
+        at = pl.multiple_of(i * 256, 256)
+        fc[mine, pl.ds(at, 256)] = nt(fm[...], onehot[pl.ds(at, 256), :]).astype(BF)
+        return carry
+
+    lax.fori_loop(0, 4, compact_step, 0)
+
+    got = exchange(0, y, to_y, lambda p: fc.at[mine, :], fc.at[mine, :])
 
     aw[y] = wt[mine, :]
     for load in loads[3:]:
@@ -234,15 +234,12 @@
         ).astype(BF)
         return carry
 
-    lax.fori_loop(0, 4, s9c_step, 0)
-
     def pick_step(i, carry):
         at = pl.multiple_of(i * 16, 16)
         ids = lax.broadcasted_iota(jnp.int32, (16, SLOTS), 0) + at
         pick[pl.ds(at, 16), :] = jnp.where(ids == spot, 1.0, 0.0).astype(BF)
         return carry
 
-    lax.fori_loop(0, 64, pick_step, 0)
     qq[...] = jnp.zeros((128, SLOTS), BF)
     gg[...] = jnp.zeros((128, SLOTS), BF)
     s1acc[...] = jnp.zeros((16, SLOTS), F32)
@@ -281,23 +278,25 @@
     def pack(i):
         s1acc[...] += nt(layer[:, span(i)], onehot[:, span(i)])
 
-    for i in range(3):
+    for i in range(4):
         expand(fc, fx, i)
+    conv(1)
+
+    def conv_step(i, carry):
+        pack(i - 1)
+        conv(i)
+        expand(fc, fx, i + 2)
+        return carry
+
+    lax.fori_loop(2, 6, conv_step, 0)
+    pack(5)
+    conv(6)
+    pack(6)
     arrive(got_hx)
     fx[:, 0:LAYER] = hx[:, 0:LAYER]
     fx[:, LAYER + CELLS : EXT] = hx[:, LAYER : 2 * LAYER]
     conv(0)
-
-    def conv_step(i, carry):
-        pack(i - 1)
-        conv(i)
-        expand(fc, fx, i + 2)
-        return carry
-
-    lax.fori_loop(1, 6, conv_step, 0)
-    pack(5)
-    conv(6)
-    pack(6)
+    pack(0)
     conv(7)
     pack(7)
     packed = s1acc[...].astype(BF)
@@ -305,6 +304,8 @@
         s1[t] = packed[:, t * 128 : t * 128 + 128]
     a1[z] = s1[z]
     got = exchange(3, z, to_z, lambda p: s1.at[p], a1.at[z])
+    lax.fori_loop(0, 64, pick_step, 0)
+    lax.fori_loop(0, 2, s9c_step, 0)
 
     drain()
     arrive(got)
@@ -323,6 +324,7 @@
     ga = nn(ow_ref[...], cw[...]).astype(BF)
     gaw[...] = ga
     gg[32:48, :] = (ga.astype(F32) * 0.25).astype(BF)
+    lax.fori_loop(2, 4, s9c_step, 0)
     arrive(got)
 
     whole = gw[...].astype(F32)

time: 108 us -> 103 us (0.954)
  Pallas kernels: 107 us -> 102 us
    pallas_call x1, Pallas kernels: 105 us -> 100 us  [body(): pl.pallas_call(whole_kernel, out_shape=(jax.ShapeDtypeStruct((16, SLOTS),...]
where the time goes in v3:
time: 103 us; the launch traced here: 102 us
  Pallas kernels  102 us (99%)
    pallas_call x1, Pallas kernels, body(): pl.pallas_call(whole_kernel, out_shape=(jax.ShapeDtypeStruct((16, SLOTS),...  100 us

profile of v3, /device:TPU:1, one launch (start us, length us, event | category | flops | bytes accessed | tf_op | source)
XLA Modules:
  0.0 102.4 jit_solution(9245413428723760091)
XLA Ops:
  0.6 100.0 %shard_map.110 = (bf16[16,1024]{1,0:T(8,128)(2,1)}, f32[16,4096]{1,0:T(8,128)}, f32[512,128]{1,0:T(8,128)}) custom-call(bf16[16,4096]{1,0:T(8,128)(2,1)} %f_in.1, s32[1,4096]{1,0:T(1,128)} %bitcast.15, s32[1,1024]{1,0:T(1,128)} %bitcast.17, bf16[16,1024]{1,0:T(8,128)(2,1)} %cot_in.1, bf16[432,128]{1,0:T(8,128)(2,1)} %bitcast.14, bf16[48,128]{1,0:T(8,128)(2,1)} %bitcast.16, ...), custom_call_target="tpu_custom_call" | custom-call | tf_op jit(solution)/shard_map/pallas_call | solution.py:602
  100.6 1.8 %shard_map.111 = (bf16[16,1024]{1,0:T(8,128)(2,1)}, f32[16,4096]{1,0:T(8,128)}, f32[432,128]{1,0:T(8,128)}, f32[48,128]{1,0:T(8,128)}, f32[16,128]{1,0:T(8,128)}) custom-call(bf16[16,1024]{1,0:T(8,128)(2,1)} %get-tuple-element.13.bo_ref, f32[16,4096]{1,0:T(8,128)} %get-tuple-element.14.gf_ref, f32[512,128]{1,0:T(8,128)} %get-tuple-element.15.vv_ref), custom_call_target="tpu_custom_call" | custom-call | tf_op jit(solution)/shard_map/pallas_call | solution.py:619

commit v4 on v3

--- a/solution.py
+++ b/solution.py
@@ -55,13 +55,13 @@
 
 def whole_kernel(
     f_in, ss_in, rs_in, cot_in, wb_in, w2_in, ow_in,
-    bo_out, gf_out, vv_out,
-    bo_ref, gf_ref, vv_ref, f_ref, ss_ref, rs_ref, cot_ref, wb_ref, w2_ref, ow_ref,
+    bo_ref, gf_ref, vv_ref,
+    f_ref, ss_ref, rs_ref, cot_ref, wb_ref, w2_ref, ow_ref,
     onehot, pick, fx, hx, hl, fm, fc, wt, aw, w9, s27, s9c, layer, s1acc,
     s1, a1, t1, a2, gw, cw, mine2, ww,
-    kvt, qq, gg, qkv, gaw, lg, pr, sc, pk, acc, big, xs, ys, u1, c2, v1, d1,
+    kvt, qq, gg, qkv, gaw, lg, pr, sc, pk, acc, big, xs, ys, u1, alive, v1, d1,
     glw, gx, hf, hl2, hg, vs, e0, half, pair, quad, own64, zsrc, zall, back64, back256,
-    in_sem, out_sem, ex_s, ex_r, halo_s, halo_r, red_s, red_r,
+    in_sem, ex_s, ex_r, halo_s, halo_r, red_s, red_r,
 ):
     z = lax.axis_index("vox_0")
     x = lax.axis_index("vox_1")
@@ -86,15 +86,6 @@
         return {"vox_0": p // 8, "vox_1": lax.rem(p, 8) // 2, "vox_2": lax.rem(p, 2)}
 
     after, before = lax.rem(d + 1, 64), lax.rem(d + 63, 64)
-
-    barrier = pltpu.get_barrier_semaphore()
-    for r in range(1, 8):
-        for me, where in ((y, to_y), (z, to_z), (xc, to_xc)):
-            pl.semaphore_signal(
-                barrier, inc=1, device_id=where(lax.rem(me + r, 8)), device_id_type=MESH
-            )
-    for p in (after, before):
-        pl.semaphore_signal(barrier, inc=1, device_id=to_d(p), device_id_type=MESH)
 
     loads = [
         pltpu.make_async_copy(src, dst, in_sem.at[i])
@@ -108,6 +99,15 @@
     for load in loads:
         load.start()
 
+    barrier = pltpu.get_barrier_semaphore()
+    for r in range(1, 8):
+        for me, where in ((y, to_y), (z, to_z), (xc, to_xc)):
+            pl.semaphore_signal(
+                barrier, inc=1, device_id=where(lax.rem(me + r, 8)), device_id_type=MESH
+            )
+    for p in (after, before):
+        pl.semaphore_signal(barrier, inc=1, device_id=to_d(p), device_id_type=MESH)
+
     fresh, old = [], []
 
     def send(src, dst, s_sem, r_sem, where):
@@ -177,15 +177,16 @@
         fc[mine, pl.ds(at, 256)] = nt(fm[...], onehot[pl.ds(at, 256), :]).astype(BF)
         return carry
 
-    lax.fori_loop(0, 4, compact_step, 0)
-
-    got = exchange(0, y, to_y, lambda p: fc.at[mine, :], fc.at[mine, :])
+
+    lax.fori_loop(0, 2, compact_step, 0)
+    got = exchange(0, y, to_y, lambda p: fc.at[mine, 0:512], fc.at[mine, 0:512])
+    lax.fori_loop(2, 4, compact_step, 0)
+    got += exchange(15, y, to_y, lambda p: fc.at[mine, 512:SLOTS], fc.at[mine, 512:SLOTS])
 
     aw[y] = wt[mine, :]
     for load in loads[3:]:
         load.wait()
     live = rs_ref[...] >= 0
-    cw[mine, :] = jnp.where(live, cot_ref[...].astype(F32), 0.0).astype(BF)
     mine2[0:48, :] = w2_ref[...]
     mine2[48:64, :] = ow_ref[...]
     ww[y] = mine2[...]
@@ -240,6 +241,13 @@
         pick[pl.ds(at, 16), :] = jnp.where(ids == spot, 1.0, 0.0).astype(BF)
         return carry
 
+    lax.fori_loop(0, 64, pick_step, 0)
+    masked = jnp.where(live, cot_ref[...].astype(F32), 0.0).astype(BF)
+    first = lax.broadcasted_iota(jnp.int32, (16, SLOTS), 0) == 0
+    moved = jnp.concatenate([masked, jnp.where(first, 1.0, 0.0).astype(BF)], axis=0)
+    moved = nt(moved, pick[...])
+    cw[mine, :] = moved[0:16].astype(BF)
+    alive[...] = moved[16:32]
     qq[...] = jnp.zeros((128, SLOTS), BF)
     gg[...] = jnp.zeros((128, SLOTS), BF)
     s1acc[...] = jnp.zeros((16, SLOTS), F32)
@@ -304,7 +312,6 @@
         s1[t] = packed[:, t * 128 : t * 128 + 128]
     a1[z] = s1[z]
     got = exchange(3, z, to_z, lambda p: s1.at[p], a1.at[z])
-    lax.fori_loop(0, 64, pick_step, 0)
     lax.fori_loop(0, 2, s9c_step, 0)
 
     drain()
@@ -316,7 +323,7 @@
     drain()
     arrive(got)
     arrived = jnp.concatenate([a2[i] for i in range(8)], axis=1)
-    gw[mine, :] = nn(arrived, pick[...]).astype(BF)
+    gw[mine, :] = arrived
     got = exchange(5, y, to_y, lambda p: gw.at[mine, :], gw.at[mine, :])
     drain()
     arrive(got_cw)
@@ -338,7 +345,7 @@
     qq[0:16, :] = (rows[0:16].astype(F32) * 0.25).astype(BF)
     row = lax.broadcasted_iota(jnp.int32, (16, SLOTS), 0)
     qq[16:32, :] = jnp.where(row == 0, 1.0, 0.0).astype(BF)
-    bias = jnp.where((row == 0) & (~live), -1e30, 0.0)
+    bias = jnp.where((row == 0) & (alive[...] < 0.5), -1e30, 0.0)
     stacked = jnp.concatenate(
         [
             rows[16:32].astype(F32),
@@ -400,7 +407,7 @@
     inverse = lax.rsqrt(var + 1e-05)
     normal = centred * inverse
     cot = cw[:, own_slots].astype(F32)
-    live_part = rs_ref[:, own_slots] >= 0
+    live_part = alive[0:1, own_slots] > 0.5
     arrive(got)
     mixed = tn(ww[:, 48:64, :].reshape(128, 128), ys[:, 0:16, :].reshape(128, 128))
     grad = None
@@ -424,19 +431,10 @@
     got = exchange(7, y, to_y, lambda p: xs.at[p], u1.at[y])
     drain()
     arrive(got)
-    grad_grouped = jnp.concatenate([u1[i, 0:16] for i in range(8)], axis=1)
-    spread = nt(grad_grouped, pick[...])
-    for t in range(8):
-        c2[t] = spread[:, t * 128 : t * 128 + 128].astype(BF)
-    v1[xc] = c2[xc]
-    got = exchange(8, xc, to_xc, lambda p: c2.at[p], v1.at[xc])
-    drain()
-    bo_ref[...] = jnp.concatenate([u1[i, 16:32] for i in range(8)], axis=1)
-    stores = [
-        pltpu.make_async_copy(src, dst, out_sem.at[i])
-        for i, (src, dst) in enumerate(((bo_ref, bo_out), (gf_ref, gf_out), (vv_ref, vv_out)))
-    ]
-    stores[0].start()
+    v1[xc] = u1[xc, 0:16, :]
+    got = exchange(8, xc, to_xc, lambda p: u1.at[p, 0:16, :], v1.at[xc])
+    drain()
+    bo_ref[...] = nn(jnp.concatenate([u1[i, 16:32] for i in range(8)], axis=1), pick[...]).astype(BF)
     arrive(got)
     for j, piece in enumerate(swap_blocks(v1[...].astype(F32))):
         d1[j] = piece.astype(BF)
@@ -522,42 +520,29 @@
     back256[rows64(x), :] = total
     got = x_send(lambda p: zall, back256.at[rows64(x), :], 4)
     lax.fori_loop(6, 8, input_step, 0)
-    stores[1].start()
+    drain()
     arrive(got)
     got = [pair_send(back256, back64, 8)]
     vv_ref[rows256(core), :] = back256[...]
     drain()
     arrive(got)
     vv_ref[rows256(1 - core), :] = back64[...]
-    stores[2].start()
-    drain()
-    drain()
-    for store in stores:
-        store.wait()
-
-
-def store_kernel(
-    bo_ref, gf_ref, vv_ref, bo_out, gf_out, gc_out, gq_out, go_out, bo, gf, vv, in_sem, out_sem
-):
-    loads = [
-        pltpu.make_async_copy(src, dst, in_sem.at[i])
-        for i, (src, dst) in enumerate(((gf_ref, gf), (vv_ref, vv), (bo_ref, bo)))
-    ]
+    drain()
+    drain()
+
+
+def store_kernel(bo_ref, gf_ref, vv_ref, bo_out, gf_out, gc_out, gq_out, go_out, sem):
     stores = [
-        pltpu.make_async_copy(src, dst, out_sem.at[i])
+        pltpu.make_async_copy(src, dst, sem.at[i])
         for i, (src, dst) in enumerate(
             (
-                (gf, gf_out), (vv.at[0:432, :], gc_out), (vv.at[432:480, :], gq_out),
-                (vv.at[480:496, :], go_out), (bo, bo_out),
+                (gf_ref, gf_out), (vv_ref.at[0:432, :], gc_out), (vv_ref.at[432:480, :], gq_out),
+                (vv_ref.at[480:496, :], go_out), (bo_ref, bo_out),
             )
         )
     ]
-    for load in loads:
-        load.start()
-    for load, behind in zip(loads, (stores[0:1], stores[1:4], stores[4:5])):
-        load.wait()
-        for store in behind:
-            store.start()
+    for store in stores:
+        store.start()
     for store in stores:
         store.wait()
 
@@ -575,7 +560,6 @@
         return pltpu.VMEM(shape, F32)
 
     scratch = [
-        buf(16, SLOTS), wide(16, CELLS), wide(512, 128),
         buf(16, CELLS), pltpu.VMEM((1, CELLS), jnp.int32), pltpu.VMEM((1, SLOTS), jnp.int32),
         buf(16, SLOTS), buf(432, 128), buf(48, 128), buf(16, 128),
         buf(SLOTS, CELLS), buf(SLOTS, SLOTS),
@@ -588,17 +572,18 @@
         buf(16, SLOTS), wide(SLOTS, 256), buf(SLOTS, 256), buf(SLOTS, 256),
         buf(64, SLOTS), wide(32, SLOTS), buf(128, SLOTS),
         buf(8, 32, 128), buf(8, 64, 128), buf(8, 32, 128),
-        buf(8, 16, 128), buf(8, 16, 128), buf(8, 16, 128),
+        wide(16, SLOTS), buf(8, 16, 128), buf(8, 16, 128),
         buf(128, SLOTS), buf(128, EXT), buf(16, 512), buf(2, 16, LAYER), buf(128, 512),
         wide(512, 128), buf(8, 16, 128), wide(256, 128), wide(256, 128),
         wide(4, 64, 128), buf(64, 128), buf(8, 64, 128), wide(64, 128),
         wide(256, 128), wide(256, 128),
-        pltpu.SemaphoreType.DMA((7,)), pltpu.SemaphoreType.DMA((3,)),
-        pltpu.SemaphoreType.DMA((15, 8)), pltpu.SemaphoreType.DMA((15, 8)),
+        pltpu.SemaphoreType.DMA((7,)),
+        pltpu.SemaphoreType.DMA((16, 8)), pltpu.SemaphoreType.DMA((16, 8)),
         pltpu.SemaphoreType.DMA((4,)), pltpu.SemaphoreType.DMA((4,)),
         pltpu.SemaphoreType.DMA((9,)), pltpu.SemaphoreType.DMA((9,)),
     ]
     hbm = pl.BlockSpec(memory_space=pltpu.HBM)
+    vmem = pl.BlockSpec(memory_space=pltpu.VMEM)
     block_out, grad_features, sums = pl.pallas_call(
         whole_kernel,
         out_shape=(
@@ -607,14 +592,19 @@
             jax.ShapeDtypeStruct((512, 128), F32),
         ),
         in_specs=[hbm] * 7,
-        out_specs=(hbm, hbm, hbm),
+        out_specs=(vmem, vmem, vmem),
         scratch_shapes=scratch,
         compiler_params=pltpu.CompilerParams(
-            collective_id=0, has_side_effects=True, vmem_limit_bytes=67043328
+            collective_id=0, has_side_effects=True, vmem_limit_bytes=48 * 1024 * 1024
         ),
     )(
-        features, send_slot.reshape(1, CELLS), recv_slot.reshape(1, SLOTS), cotangent,
-        wb, w2, out_weight,
+        *(
+            pltpu.with_memory_space_constraint(array, pltpu.HBM)
+            for array in (
+                features, send_slot.reshape(1, CELLS), recv_slot.reshape(1, SLOTS), cotangent,
+                wb, w2, out_weight,
+            )
+        )
     )
     block_out, grad_features, grad_conv, grad_qkv, grad_out = pl.pallas_call(
         store_kernel,
@@ -625,13 +615,10 @@
             jax.ShapeDtypeStruct((48, 128), F32),
             jax.ShapeDtypeStruct((16, 128), F32),
         ),
-        in_specs=[hbm] * 3,
+        in_specs=[vmem] * 3,
         out_specs=(hbm,) * 5,
-        scratch_shapes=[
-            buf(16, SLOTS), wide(16, CELLS), wide(512, 128),
-            pltpu.SemaphoreType.DMA((3,)), pltpu.SemaphoreType.DMA((5,)),
-        ],
-        compiler_params=pltpu.CompilerParams(vmem_limit_bytes=67043328),
+        scratch_shapes=[pltpu.SemaphoreType.DMA((5,))],
+        compiler_params=pltpu.CompilerParams(vmem_limit_bytes=4 * 1024 * 1024),
     )(block_out, grad_features, sums)
     grad_conv = jnp.transpose(grad_conv.reshape(27, 16, 128), (0, 2, 1))
     grad_qkv = jnp.transpose(grad_qkv.reshape(3, 16, 128), (0, 2, 1))

time: 103 us -> 101 us (0.981)
  Pallas kernels: 102 us -> 100 us
where the time goes in v4:
time: 101 us
  Pallas kernels  100 us (99%)
    pallas_call x1, Pallas kernels, body(): pl.pallas_call(whole_kernel, out_shape=(jax.ShapeDtypeStruct((16, SLOTS),...  99.3 us

profile of v4, /device:TPU:1, one launch (start us, length us, event | category | flops | bytes accessed | tf_op | source)
XLA Modules:
  0.0 100.8 jit_solution(11586892393471366401)
XLA Ops:
  0.6 99.3 %shard_map.110 = (bf16[16,1024]{1,0:T(8,128)(2,1)S(1)}, f32[16,4096]{1,0:T(8,128)S(1)}, f32[512,128]{1,0:T(8,128)S(1)}) custom-call(bf16[16,4096]{1,0:T(8,128)(2,1)} %f_in.1, s32[1,4096]{1,0:T(1,128)} %bitcast.15, s32[1,1024]{1,0:T(1,128)} %bitcast.17, bf16[16,1024]{1,0:T(8,128)(2,1)} %cot_in.1, bf16[432,128]{1,0:T(8,128)(2,1)} %bitcast.14, ...), custom_call_target="tpu_custom_call" | custom-call | tf_op jit(solution)/shard_map/pallas_call | solution.py:587
  99.9 0.8 shard_map.111

commit v5 on v4

--- a/solution.py
+++ b/solution.py
@@ -61,6 +61,7 @@
     s1, a1, t1, a2, gw, cw, mine2, ww,
     kvt, qq, gg, qkv, gaw, lg, pr, sc, pk, acc, big, xs, ys, u1, alive, v1, d1,
     glw, gx, hf, hl2, hg, vs, e0, half, pair, quad, own64, zsrc, zall, back64, back256,
+    pattern, high,
     in_sem, ex_s, ex_r, halo_s, halo_r, red_s, red_r,
 ):
     z = lax.axis_index("vox_0")
@@ -150,10 +151,14 @@
     mine = rows16(y)
     loads[0].wait()
 
+    low = lax.broadcasted_iota(jnp.int32, (16, CELLS), 0)
+    pattern[...] = jnp.where(low == (ss_ref[...] & 15), 1.0, 0.0).astype(BF)
+    high[...] = jnp.broadcast_to((ss_ref[...] >> 4).astype(F32), (16, CELLS)).astype(BF)
+
     def onehot_step(i, carry):
         at = pl.multiple_of(i * 16, 16)
-        ids = lax.broadcasted_iota(jnp.int32, (16, CELLS), 0) + at
-        onehot[pl.ds(at, 16), :] = jnp.where(ids == ss_ref[...], 1.0, 0.0).astype(BF)
+        here = high[...] == i.astype(F32).astype(BF)
+        onehot[pl.ds(at, 16), :] = jnp.where(here, pattern[...], jnp.zeros((), BF))
         return carry
 
     lax.fori_loop(0, 64, onehot_step, 0)
@@ -498,13 +503,16 @@
 
     got = [pair_send(vs.at[rows256(1 - core), :], half, 0)]
     arrive(got)
-    pair[...] = vs[rows256(core), :] + half[...]
+    pair[...] = (vs[rows256(core), :] + half[...]).astype(BF)
     quad[x] = pair[rows64(x), :]
     got = x_send(lambda p: pair.at[rows64(p), :], quad.at[x], 0)
     drain()
     lax.fori_loop(0, 8, grad_expand, 0)
     arrive(got)
-    own64[...] = (quad[0] + quad[1] + quad[2] + quad[3]).astype(BF)
+    total = quad[0].astype(F32)
+    for i in range(1, 4):
+        total = total + quad[i].astype(F32)
+    own64[...] = total.astype(BF)
     zsrc[z] = own64[...]
     got = exchange(14, z, to_z, lambda p: own64, zsrc.at[z])
     drain()
@@ -516,17 +524,17 @@
     total = zsrc[0].astype(F32)
     for i in range(1, 8):
         total = total + zsrc[i].astype(F32)
-    zall[...] = total
-    back256[rows64(x), :] = total
+    zall[...] = total.astype(BF)
+    back256[rows64(x), :] = zall[...]
     got = x_send(lambda p: zall, back256.at[rows64(x), :], 4)
     lax.fori_loop(6, 8, input_step, 0)
     drain()
     arrive(got)
     got = [pair_send(back256, back64, 8)]
-    vv_ref[rows256(core), :] = back256[...]
-    drain()
-    arrive(got)
-    vv_ref[rows256(1 - core), :] = back64[...]
+    vv_ref[rows256(core), :] = back256[...].astype(F32)
+    drain()
+    arrive(got)
+    vv_ref[rows256(1 - core), :] = back64[...].astype(F32)
     drain()
     drain()
 
@@ -574,9 +582,10 @@
         buf(8, 32, 128), buf(8, 64, 128), buf(8, 32, 128),
         wide(16, SLOTS), buf(8, 16, 128), buf(8, 16, 128),
         buf(128, SLOTS), buf(128, EXT), buf(16, 512), buf(2, 16, LAYER), buf(128, 512),
-        wide(512, 128), buf(8, 16, 128), wide(256, 128), wide(256, 128),
-        wide(4, 64, 128), buf(64, 128), buf(8, 64, 128), wide(64, 128),
-        wide(256, 128), wide(256, 128),
+        wide(512, 128), buf(8, 16, 128), wide(256, 128), buf(256, 128),
+        buf(4, 64, 128), buf(64, 128), buf(8, 64, 128), buf(64, 128),
+        buf(256, 128), buf(256, 128),
+        buf(16, CELLS), buf(16, CELLS),
         pltpu.SemaphoreType.DMA((7,)),
         pltpu.SemaphoreType.DMA((16, 8)), pltpu.SemaphoreType.DMA((16, 8)),
         pltpu.SemaphoreType.DMA((4,)), pltpu.SemaphoreType.DMA((4,)),

time: 101 us -> 100 us (0.990)
  no operation moved by 1% of the time
where the time goes in v5:
time: 100 us
  Pallas kernels  99.3 us (99%)
    pallas_call x1, Pallas kernels, body(): pl.pallas_call(whole_kernel, out_shape=(jax.ShapeDtypeStruct((16, SLOTS),...  98.5 us

profile of v5, /device:TPU:1, one launch (start us, length us, event | category | flops | bytes accessed | tf_op | source)
XLA Modules:
  0.0 100.0 jit_solution(1474074830625675449)
XLA Ops:
  0.6 98.5 %shard_map.110 = (bf16[16,1024]{1,0:T(8,128)(2,1)S(1)}, f32[16,4096]{1,0:T(8,128)S(1)}, f32[512,128]{1,0:T(8,128)S(1)}) custom-call(bf16[16,4096]{1,0:T(8,128)(2,1)} %f_in.1, s32[1,4096]{1,0:T(1,128)} %bitcast.15, s32[1,1024]{1,0:T(1,128)} %bitcast.17, bf16[16,1024]{1,0:T(8,128)(2,1)} %cot_in.1, bf16[432,128]{1,0:T(8,128)(2,1)} %bitcast.14, ...), custom_call_target="tpu_custom_call" | custom-call | tf_op jit(solution)/shard_map/pallas_call | solution.py:596
  99.1 0.8 shard_map.111

commit v6 on v5

--- a/solution.py
+++ b/solution.py
@@ -183,10 +183,8 @@
         return carry
 
 
-    lax.fori_loop(0, 2, compact_step, 0)
-    got = exchange(0, y, to_y, lambda p: fc.at[mine, 0:512], fc.at[mine, 0:512])
-    lax.fori_loop(2, 4, compact_step, 0)
-    got += exchange(15, y, to_y, lambda p: fc.at[mine, 512:SLOTS], fc.at[mine, 512:SLOTS])
+    lax.fori_loop(0, 4, compact_step, 0)
+    got = exchange(0, y, to_y, lambda p: fc.at[mine, :], fc.at[mine, :])
 
     aw[y] = wt[mine, :]
     for load in loads[3:]:

time: 100 us -> 99.4 us (level)
  no operation moved by 1% of the time
where the time goes in v6:
time: 99.4 us; the launch traced here: 99.2 us
  Pallas kernels  98.6 us (99%)
    pallas_call x1, Pallas kernels, body(): pl.pallas_call(whole_kernel, out_shape=(jax.ShapeDtypeStruct((16, SLOTS),...  97.7 us

profile of v6, /device:TPU:1, one launch (start us, length us, event | category | flops | bytes accessed | tf_op | source)
XLA Modules:
  0.0 99.2 jit_solution(17193809725329584020)
XLA Ops:
  0.6 97.7 %shard_map.110 = (bf16[16,1024]{1,0:T(8,128)(2,1)S(1)}, f32[16,4096]{1,0:T(8,128)S(1)}, f32[512,128]{1,0:T(8,128)S(1)}) custom-call(bf16[16,4096]{1,0:T(8,128)(2,1)} %f_in.1, s32[1,4096]{1,0:T(1,128)} %bitcast.15, s32[1,1024]{1,0:T(1,128)} %bitcast.17, bf16[16,1024]{1,0:T(8,128)(2,1)} %cot_in.1, bf16[432,128]{1,0:T(8,128)(2,1)} %bitcast.14, ...), custom_call_target="tpu_custom_call" | custom-call | tf_op jit(solution)/shard_map/pallas_call | solution.py:594
  98.4 0.8 shard_map.111
